TPU v7x, 32 devices: a whole 2x2x4 slice. The times are simulated.
32 devices in a mesh: grp: 2 (over y), tile: 4 (over z), rep: 4 (over x, core).
Axes of the slice: x: 2, y: 2, z: 4, core: 2. Of those that a mesh axis runs over, the one named last changes fastest.
Arguments:
- focusing: bfloat16 [2, 512, 1024], P(None, 'grp', 'tile'), parts along dimension 1, may hold values from -6 to 6
- source_basis: bfloat16 [2, 64, 8, 1024], P(None, 'rep', 'grp', 'tile'), parts along dimension 2, may hold values from -0.375 to 0.375
- receiver_basis: bfloat16 [2, 64, 8, 1024], P(None, 'rep', 'grp', 'tile'), parts along dimension 2, may hold values from -0.21875 to 0.21875
- tile_ranks: int32 [8, 4], P('grp', 'tile'), parts along dimension 0, may hold values from 1 to 4
- keep_counts: int32 [8], P(('grp', 'tile')), parts along dimension 0, may hold values from 64 to 256
Outputs:
- forward_data: float32 [2, 512, 1024], P(None, ('grp', 'rep'), 'tile'), parts along dimension 1
- muted_adjoint_result: float32 [2, 512, 1024], P(None, ('grp', 'rep'), 'tile'), parts along dimension 1
- correlations: float32 [2, 256, 512], P(None, 'rep', 'grp'), parts along dimension 2
There are 2 independent parts, one for each index of `grp`. A program takes and returns all parts, laid end to end along the dimension named above; each array names one. Nothing has to cross between parts.
Inputs may be any that keep to these rules, and one draw needn't show every extreme that they name: `tile_ranks`: number of live buckets of 16 ranks in each tile. `keep_counts`: receivers kept in each receiver tile, counted from its first position.
All inputs are finite; a program needn't handle non-finite values.
Results may differ from a plain program's by a relative error of at most 0.0039.
Values may be sent and summed in bfloat16 or wider, within the bound.
No kernel may reach another device: no remote copies, remote signals or barrier semaphores. Data moves between devices by JAX's collectives and lax.ppermute only.
A program may use at most 64 MiB of HBM per device.

v0:
```python
import math

import jax
import jax.numpy as jnp
from jax import lax
from jax.sharding import PartitionSpec as P

SPAN = 256
BUCKET = 16
FOC = 256


def bucket_live(rank_column, local_tile_ranks):
    bucket_index = lax.iota(jnp.int32, local_tile_ranks) // BUCKET
    return bucket_index[:, None] < rank_column[None, :]


def forward_coefficients(basis_here, focal_here, live_mask):
    local_tile_ranks = basis_here.shape[1]
    row_tiles = basis_here.shape[2]
    width_here = basis_here.shape[3]
    points_here = focal_here.shape[1]
    product = lax.dot_general(
        basis_here.reshape(2 * local_tile_ranks * row_tiles, width_here),
        focal_here.reshape(2 * points_here, width_here),
        (((1,), (1,)), ((), ())),
        preferred_element_type=jnp.float32,
    )
    product = product.reshape(2, local_tile_ranks, row_tiles, 2, points_here)
    real_part = product[0, :, :, 0] - product[1, :, :, 1]
    imag_part = product[0, :, :, 1] + product[1, :, :, 0]
    stacked = jnp.where(live_mask[None, :, :, None], jnp.stack([real_part, imag_part]), 0.0)
    return stacked.astype(jnp.bfloat16).reshape(2, local_tile_ranks, row_tiles, 1, points_here)


def forward_regroup(coefficient, lifting):
    local_tile_ranks = lifting.shape[1]
    col_tiles = lifting.shape[2]
    width_here = lifting.shape[3]
    flattened_lifting = lifting.reshape(2, local_tile_ranks * col_tiles, width_here)
    arrived = lax.all_to_all(coefficient, "tile", split_axis=2, concat_axis=3, tiled=True)
    item_count = arrived.shape[4]
    received_flattened = arrived.reshape(2, local_tile_ranks * col_tiles, item_count)
    blocks = jnp.einsum(
        "wgh,lgj->wlhj", received_flattened, flattened_lifting, preferred_element_type=jnp.float32
    )
    return jnp.stack([blocks[0, 0] - blocks[1, 1], blocks[1, 0] + blocks[0, 1]])


def adjoint_coefficients(lifting, masked):
    local_tile_ranks = lifting.shape[1]
    col_tiles = lifting.shape[2]
    width_here = lifting.shape[3]
    points_here = masked.shape[1]
    blocks = jnp.einsum(
        "pks,qfs->pqkf",
        lifting.reshape(2, local_tile_ranks * col_tiles, width_here),
        masked,
        preferred_element_type=jnp.float32,
    )
    stacked = jnp.stack([blocks[0, 0] + blocks[1, 1], blocks[0, 1] - blocks[1, 0]])
    return stacked.astype(jnp.bfloat16).reshape(2, local_tile_ranks, 1, col_tiles, points_here)


def adjoint_regroup(coefficient, basis_here, live_mask):
    local_tile_ranks = basis_here.shape[1]
    row_tiles = basis_here.shape[2]
    width_here = basis_here.shape[3]
    flattened_basis = basis_here.reshape(2, local_tile_ranks * row_tiles, width_here)
    arrived = lax.all_to_all(coefficient, "tile", split_axis=3, concat_axis=2, tiled=True)
    item_count = arrived.shape[4]
    kept_rows = jnp.where(live_mask[None, :, :, None, None], arrived, jnp.zeros((), jnp.bfloat16))
    received_flattened = kept_rows.reshape(2, local_tile_ranks * row_tiles, item_count)
    blocks = jnp.einsum(
        "wgh,lgj->wlhj", received_flattened, flattened_basis, preferred_element_type=jnp.float32
    )
    return jnp.stack([blocks[0, 0] + blocks[1, 1], blocks[1, 0] - blocks[0, 1]])


def correlate(image_part, focusing, factor):
    blocks = jnp.einsum(
        "pgs,qfs->pqgf",
        image_part,
        focusing.astype(jnp.float32),
        precision=lax.Precision.HIGHEST,
        preferred_element_type=jnp.float32,
    )
    return factor * jnp.stack([blocks[0, 0] + blocks[1, 1], blocks[1, 0] - blocks[0, 1]])


def per_device(focusing, source_basis, receiver_basis, tile_ranks, keep_counts):
    width_here = focusing.shape[2]
    portion_count = FOC // lax.axis_size("rep")
    rep_index = lax.axis_index("rep")
    column = tile_ranks[:, 0]
    weights = (lax.iota(jnp.int32, width_here) < keep_counts[0]).astype(jnp.float32)
    order_total = width_here * lax.axis_size("tile")
    factor = 1.0 / math.sqrt(SPAN * order_total)
    every_source, receiver_all = (
        lax.all_gather(source_basis, "rep", axis=1, tiled=True),
        lax.all_gather(receiver_basis, "rep", axis=1, tiled=True),
    )
    focal_share = lax.dynamic_slice_in_dim(focusing, rep_index * portion_count, portion_count, 1)
    live_mask = bucket_live(column, every_source.shape[1])
    coefficient = forward_coefficients(every_source, focal_share, live_mask)
    forward_data = forward_regroup(coefficient, receiver_all)
    masked = (forward_data * weights).astype(jnp.bfloat16)
    muted_adjoint_result = adjoint_regroup(
        adjoint_coefficients(receiver_all, masked), every_source, live_mask
    )
    correlations = lax.psum(correlate(muted_adjoint_result, focusing, factor), "tile")
    return (forward_data, muted_adjoint_result, correlations)


def solution(mesh):
    placed = (
        P(None, "grp", "tile"),
        P(None, "rep", "grp", "tile"),
        P(None, "rep", "grp", "tile"),
        P("grp", "tile"),
        P(("grp", "tile")),
    )
    return jax.shard_map(
        per_device,
        mesh=mesh,
        in_specs=placed,
        out_specs=(
            P(None, ("grp", "rep"), "tile"),
            P(None, ("grp", "rep"), "tile"),
            P(None, "rep", "grp"),
        ),
        check_vma=False,
    )
```

profile of v0, /device:TPU:0, one launch (start us, length us, event | category | flops | bytes accessed | tf_op | source)
XLA Modules:
  0.0 86.6 jit_solution(12190605883118274594)
XLA Ops:
  7.2 7.6 %all_gather.6 = bf16[2,64,4,256]{3,2,1,0:T(4,128)(2,1)S(1)} all-gather(bf16[2,16,4,256]{3,2,1,0:T(4,128)(2,1)} %param.6), channel_id=1, replica_groups=mesh['grp'=2,'tile'=4,'rep'=4] {'rep'}, dimensions={1}, use_global_device_ids=true | all-gather | bytes 327680 | tf_op jit(solution)/shard_map/all_gather | solution.py:100
  14.9 0.2 convolution_bitcast_fusion.4
  15.1 0.1 copy.25
  15.2 0.3 reshape.368
  15.6 0.3 slice_subtract_fusion
  15.9 0.6 copy-done.4
  16.7 0.5 fusion
  17.3 0.8 reshape.381
  18.1 5.0 %all-to-all-start = ((bf16[4,2,4096]{2,1,0:T(2,128)(2,1)}), bf16[4,2,4096]{2,1,0:T(2,128)(2,1)S(1)}, u32[]{:S(2)}, u32[]{:S(2)}) async-start(bf16[4,2,4096]{2,1,0:T(2,128)(2,1)} %reshape.381), calls=%async_computation | async-start | bytes 131072 | tf_op jit(solution)/shard_map/all_to_all | solution.py:41
  23.1 5.8 %all_gather.7 = bf16[2,64,4,256]{3,2,1,0:T(4,128)(2,1)S(1)} all-gather(bf16[2,16,4,256]{3,2,1,0:T(4,128)(2,1)S(1)} %copy-done.3), channel_id=1, replica_groups=mesh['grp'=2,'tile'=4,'rep'=4] {'rep'}, dimensions={1}, use_global_device_ids=true | all-gather | bytes 327680 | tf_op jit(solution)/shard_map/all_gather | solution.py:101
  29.6 0.1 reshape.382
  29.9 0.2 convolution_bitcast_fusion.2
  30.2 0.2 convolution_bitcast_fusion.3
  30.4 0.4 copy-done.1
  31.2 0.8 reshape.383
  32.0 5.1 %all-to-all-start.1 = ((bf16[4,2,4096]{2,1,0:T(2,128)(2,1)}), bf16[4,2,4096]{2,1,0:T(2,128)(2,1)S(1)}, u32[]{:S(2)}, u32[]{:S(2)}) async-start(bf16[4,2,4096]{2,1,0:T(2,128)(2,1)} %reshape.383), calls=%async_computation.1 | async-start | bytes 131072 | tf_op jit(solution)/shard_map/all_to_all | solution.py:70
  37.2 5.7 %all-to-all-done.1 = bf16[4,2,4096]{2,1,0:T(2,128)(2,1)S(1)} async-done(((bf16[4,2,4096]{2,1,0:T(2,128)(2,1)}), bf16[4,2,4096]{2,1,0:T(2,128)(2,1)S(1)}, u32[]{:S(2)}, u32[]{:S(2)}) %all-to-all-start.1) | async-done | bytes 65568 | tf_op jit(solution)/shard_map/all_to_all | solution.py:70
  42.9 0.1 reshape.384
  43.2 0.2 convolution_bitcast_fusion.1
  43.5 0.4 convolution_bitcast_fusion
  43.9 0.2 copy-done.2
  44.2 0.7 maximum_multiply_fusion
  44.8 33.4 %all-reduce.2.cloned.1.call-done = f32[2,64,256]{2,1,0:T(8,128)} async-done(((f32[2,64,256]{2,1,0:T(8,128)}), f32[2,64,256]{2,1,0:T(8,128)}) %all-reduce.2.cloned.1.call-update) | async-done | bytes 131088 | tf_op jit(solution)/shard_map/psum | solution.py:111
  78.2 1.6 %copy.48 = f32[2,64,256]{2,1,0:T(8,128)} copy(f32[2,64,256]{2,1,0:T(8,128)} %all-reduce.2.cloned.1.call-done) | data formatting | bytes 262144
  (32 shorter events, 1.3 us)
Async XLA Ops:
  7.2 7.7 %copy-start = (bf16[2,256,256]{2,1,0:T(8,128)(2,1)S(1)}, bf16[2,256,256]{2,1,0:T(8,128)(2,1)}, u32[]{:S(2)}) copy-start(bf16[2,256,256]{2,1,0:T(8,128)(2,1)} %param.5) | copy-start | bytes 786436
  15.9 0.7 copy-start.4
  18.1 5.0 %copy-start.3 = (bf16[2,16,4,256]{3,2,1,0:T(4,128)(2,1)S(1)}, bf16[2,16,4,256]{3,2,1,0:T(4,128)(2,1)}, u32[]{:S(2)}) copy-start(bf16[2,16,4,256]{3,2,1,0:T(4,128)(2,1)} %param.7) | copy-start | bytes 196612
  18.1 11.5 %all-to-all-start = ((bf16[4,2,4096]{2,1,0:T(2,128)(2,1)}), bf16[4,2,4096]{2,1,0:T(2,128)(2,1)S(1)}, u32[]{:S(2)}, u32[]{:S(2)}) async-start(bf16[4,2,4096]{2,1,0:T(2,128)(2,1)} %reshape.381), calls=%async_computation | async-start | bytes 131072 | tf_op jit(solution)/shard_map/all_to_all | solution.py:41
  30.2 0.7 copy-start.1
  32.0 10.8 %all-to-all-start.1 = ((bf16[4,2,4096]{2,1,0:T(2,128)(2,1)}), bf16[4,2,4096]{2,1,0:T(2,128)(2,1)S(1)}, u32[]{:S(2)}, u32[]{:S(2)}) async-start(bf16[4,2,4096]{2,1,0:T(2,128)(2,1)} %reshape.383), calls=%async_computation.1 | async-start | bytes 131072 | tf_op jit(solution)/shard_map/all_to_all | solution.py:70
  37.1 41.1 %all-reduce.2.cloned.1.call-start = ((), (), s32[]{:S(2)}) async-start(), calls=%async_computation.2 | async-start | bytes 262144 | tf_op jit(solution)/shard_map/psum | solution.py:111
  43.5 0.7 copy-start.2
Sparse Core Ops, SparseCore 0:
  45.0 33.1 all-reduce.1
where the time goes:
time: 87.1 us; the launch traced here: 86.6 us
  waiting for transfers between devices  39.1 us (45%)
  between operations  14.9 us (17%)
  blocking collectives  13.3 us (15%)
  starting transfers between devices  10.1 us (12%)
  local copies, waits for them, and re-layouts  6.04 us (7%)
  other arithmetic  1.89 us (2%)
  matrix products  1.25 us (1%)
    psum x1, waiting for transfers between devices, per_device(): lax.psum(correlate(muted_adjoint_result, focusing, factor), 'tile')  33.4 us
    all_gather x1, blocking collectives, per_device(): lax.all_gather(source_basis, 'rep', axis=1, tiled=True)  7.57 us
    all_gather x1, blocking collectives, per_device(): lax.all_gather(receiver_basis, 'rep', axis=1, tiled=True)  5.76 us
    all_to_all x1, waiting for transfers between devices, adjoint_regroup(): lax.all_to_all(coefficient, 'tile', split_axis=3, concat_axis=2, tiled=True)  5.67 us
    all_to_all x1, starting transfers between devices, adjoint_regroup(): lax.all_to_all(coefficient, 'tile', split_axis=3, concat_axis=2, tiled=True)  5.09 us
    all_to_all x1, starting transfers between devices, forward_regroup(): lax.all_to_all(coefficient, 'tile', split_axis=2, concat_axis=3, tiled=True)  5.03 us
    unnamed x15, local copies, waits for them, and re-layouts  4.78 us
  transfers between devices with their start and end apart: 3, of which 2 were waited for; matrix products, arithmetic and copies ran while one was open for 0% of the time, Pallas kernels for 0%

commit v1 on v0

v1 whole, which is shorter than its diff:
```python
import functools
import math

import jax
import jax.numpy as jnp
from jax import lax
from jax.experimental import pallas as pl
from jax.experimental.pallas import tpu as pltpu
from jax.sharding import PartitionSpec as P


SPAN = 256
BUCKET = 16
BF16 = jnp.bfloat16
F32 = jnp.float32

NT = (((1,), (1,)), ((), ()))
NN = (((1,), (0,)), ((), ()))
TN = (((0,), (0,)), ((), ()))


def dot(a, b, dims):
    return lax.dot_general(a, b, dims, preferred_element_type=F32)


def swap(x, axis, step):
    count = lax.axis_size(axis)
    return lax.ppermute(x, axis, [(i, i ^ step) for i in range(count)])


LANES = 128


def fold(ref, start, value):
    rows, columns = value.shape
    for part in range(columns // LANES):
        ref[part, pl.ds(start, rows), :] = value[:, part * LANES : (part + 1) * LANES]


def every(ref, start, count, stride):
    parts = [ref[part, pl.ds(start, count, stride=stride), :] for part in range(ref.shape[0])]
    return jnp.concatenate(parts, axis=1)


def live_rows(ranks_ref, cell, shard, ranks):
    rows = lax.broadcasted_iota(jnp.int32, (ranks, 1), 0) + shard * ranks
    return rows < ranks_ref[cell, 0] * BUCKET


def forward_kernel(ranks_ref, basis_ref, foc_ref, *refs, tiles, ranks):
    outs, made, blocks = refs[:tiles], refs[tiles], refs[tiles + 1]
    here = lax.axis_index("tile")
    shard = lax.axis_index("rep")
    half = ranks * tiles
    points = foc_ref.shape[0] // 2
    prod = dot(basis_ref[...], foc_ref[...], NT)
    fold(made, 0, prod[:half, :points] - prod[half:, points:])
    fold(made, half, prod[:half, points:] + prod[half:, :points])
    for cell in range(tiles):
        mask = live_rows(ranks_ref, cell, shard, ranks)
        for part in range(2):
            rows = every(made, part * half + cell, ranks, tiles)
            blocks[cell, pl.ds(part * ranks, ranks), :] = jnp.where(mask, rows, 0.0).astype(BF16)
    for step in range(tiles):
        outs[step][...] = blocks[here ^ step]


def lift_kernel(keep_ref, *refs, tiles, reps, ranks):
    pieces, out, weight, wide = refs[:reps], refs[reps], refs[reps + 1], refs[reps + 2]
    here = lax.axis_index("tile")
    half = ranks * tiles
    width = pieces[0].shape[1]
    columns = lax.broadcasted_iota(jnp.int32, weight.shape, 1)
    columns = jnp.where(columns >= width, columns - width, columns)
    weight[...] = (columns < keep_ref[0]).astype(F32)
    for shard in range(reps):
        fold(wide, 0, pieces[shard][...].astype(F32))
        for cell in range(tiles):
            real = every(wide, cell, ranks, tiles)
            imag = every(wide, half + cell, ranks, tiles)
            spot = here ^ cell
            out[spot, shard, pl.ds(0, ranks), pl.ds(0, width)] = real.astype(BF16)
            out[spot, shard, pl.ds(0, ranks), pl.ds(width, width)] = imag.astype(BF16)
            out[spot, shard, pl.ds(ranks, ranks), pl.ds(0, width)] = (-imag).astype(BF16)
            out[spot, shard, pl.ds(ranks, ranks), pl.ds(width, width)] = real.astype(BF16)


def image_basis_kernel(ranks_ref, *refs, tiles, reps, ranks):
    pieces, out, wide = refs[:reps], refs[reps], refs[reps + 1]
    here = lax.axis_index("tile")
    me = lax.axis_index("rep")
    half = ranks * tiles
    width = pieces[0].shape[1]
    for shard in range(reps):
        fold(wide, 0, pieces[shard][...].astype(F32))
        for cell in range(tiles):
            mask = live_rows(ranks_ref, cell, me ^ shard, ranks)
            real = jnp.where(mask, every(wide, cell, ranks, tiles), 0.0)
            imag = jnp.where(mask, every(wide, half + cell, ranks, tiles), 0.0)
            spot = here ^ cell
            out[spot, shard, pl.ds(0, ranks), pl.ds(0, width)] = real.astype(BF16)
            out[spot, shard, pl.ds(0, ranks), pl.ds(width, width)] = (-imag).astype(BF16)
            out[spot, shard, pl.ds(ranks, ranks), pl.ds(0, width)] = imag.astype(BF16)
            out[spot, shard, pl.ds(ranks, ranks), pl.ds(width, width)] = real.astype(BF16)


def middle_kernel(*refs, tiles, reps, factor):
    pieces, lift_ref, weight_ref = refs[:reps], refs[reps], refs[reps + 1]
    fwd_out, own_corr, own_back = refs[reps + 2], refs[reps + 3], refs[reps + 4]
    sends, whole = refs[reps + 5 : reps + 4 + tiles], refs[reps + 4 + tiles]
    me = lax.axis_index("rep")
    points, width2 = whole.shape
    width = width2 // 2
    share = points // reps
    block = lift_ref.shape[2]
    total = None
    for shard in range(reps):
        lift = lift_ref[:, shard].reshape(tiles * block, width2)
        part = dot(pieces[shard][...], lift, TN)
        total = part if total is None else total + part
    whole[...] = total
    mine = whole[pl.ds(pl.multiple_of(me * share, share), share), :]
    fwd_out[0] = mine[:, :width]
    fwd_out[1] = mine[:, width:]
    muted = (mine * weight_ref[pl.ds(0, 1), :]).astype(BF16)
    back = dot(muted, lift_ref[...].reshape(tiles * reps * block, width2), NT).astype(BF16)
    cell = reps * block
    high = total.astype(BF16)
    low = (total - high.astype(F32)).astype(BF16)
    turned = jnp.concatenate([muted[:, width:], -muted[:, :width]], axis=1)
    left = jnp.concatenate([muted, turned], axis=0)
    corr = (dot(left, high, NT) + dot(left, low, NT)) * factor
    own_corr[...] = corr
    own_back[...] = back[:, :cell]
    small = corr.astype(BF16)
    for step in range(1, tiles):
        out = sends[step - 1]
        out[pl.ds(0, 2 * share), :] = small
        piece = back[:, step * cell : (step + 1) * cell]
        out[pl.ds(2 * share, share // 2), pl.ds(0, cell)] = piece[: share // 2]
        out[pl.ds(2 * share, share // 2), pl.ds(cell, cell)] = piece[share // 2 :]


def final_kernel(*refs, tiles, reps):
    own_corr, own_back, basis_ref = refs[:3]
    arrived = refs[3 : 2 + tiles]
    adj_out, corr_out, back = refs[2 + tiles :]
    share = own_back.shape[0]
    cell = own_back.shape[1]
    width2 = basis_ref.shape[3]
    width = width2 // 2
    block = basis_ref.shape[2]
    back[:, pl.ds(0, cell)] = own_back[...]
    corr = own_corr[...]
    for step in range(1, tiles):
        got = arrived[step - 1]
        corr = corr + got[pl.ds(0, 2 * share), :].astype(F32)
        back[pl.ds(0, share // 2), pl.ds(step * cell, cell)] = got[pl.ds(2 * share, share // 2), pl.ds(0, cell)]
        back[pl.ds(share // 2, share // 2), pl.ds(step * cell, cell)] = got[pl.ds(2 * share, share // 2), pl.ds(cell, cell)]
    image = dot(back[...], basis_ref[...].reshape(tiles * reps * block, width2), NN)
    adj_out[0] = image[:, :width]
    adj_out[1] = image[:, width:]
    corr_out[0] = corr[:share]
    corr_out[1] = corr[share:]


def call(kernel, ins, outs, scratch, args):
    vmem, smem = pl.BlockSpec(memory_space=pltpu.VMEM), pl.BlockSpec(memory_space=pltpu.SMEM)
    return pl.pallas_call(
        kernel,
        in_specs=[smem if kind == "s" else vmem for kind in ins],
        out_specs=jax.tree.map(lambda _: vmem, outs),
        out_shape=outs,
        scratch_shapes=scratch,
    )(*args)


def short_path(focusing, source_basis, receiver_basis, tile_ranks, keep_counts):
    tiles, reps = lax.axis_size("tile"), lax.axis_size("rep")
    ranks, width = source_basis.shape[1], source_basis.shape[3]
    points = focusing.shape[1]
    share = points // reps
    block = 2 * ranks
    factor = 1.0 / math.sqrt(SPAN * width * tiles)
    shaped = jax.ShapeDtypeStruct
    order = sorted(range(1, tiles), reverse=True)
    rep_order = sorted(range(1, reps), key=lambda s: (s == 1, s))

    source = source_basis.reshape(2 * ranks * tiles, width)
    receiver = receiver_basis.reshape(2 * ranks * tiles, width)
    made = call(
        functools.partial(forward_kernel, tiles=tiles, ranks=ranks),
        "svv",
        [shaped((block, points), BF16)] * tiles,
        [pltpu.VMEM((points // LANES, block * tiles, LANES), F32), pltpu.VMEM((tiles, block, points), BF16)],
        (tile_ranks, source, focusing.reshape(2 * points, width)),
    )
    got = {step: swap(made[step], "tile", step) for step in order}
    lifts = {step: swap(receiver, "rep", step) for step in rep_order}
    gathered = jnp.concatenate([made[0]] + [got[step] for step in range(1, tiles)], axis=0)
    spread = {step: swap(gathered, "rep", step) for step in rep_order}
    lift, weight = call(
        functools.partial(lift_kernel, tiles=tiles, reps=reps, ranks=ranks),
        "s" + "v" * reps,
        [shaped((tiles, reps, block, 2 * width), BF16), shaped((8, 2 * width), F32)],
        [pltpu.VMEM((width // LANES, block * tiles, LANES), F32)],
        (keep_counts, receiver, *[lifts[step] for step in range(1, reps)]),
    )
    middle = call(
        functools.partial(middle_kernel, tiles=tiles, reps=reps, factor=factor),
        "v" * (reps + 2),
        [shaped((2, share, width), F32), shaped((2 * share, points), F32), shaped((share, reps * block), BF16)]
        + [shaped((2 * share + share // 2, points), BF16)] * (tiles - 1),
        [pltpu.VMEM((points, 2 * width), F32)],
        (gathered, *[spread[step] for step in range(1, reps)], lift, weight),
    )
    forward_data, own_corr, own_back = middle[:3]
    sent = {step: swap(middle[2 + step], "tile", step) for step in order}
    bases = {step: swap(source, "rep", step) for step in rep_order}
    basis = call(
        functools.partial(image_basis_kernel, tiles=tiles, reps=reps, ranks=ranks),
        "s" + "v" * reps,
        shaped((tiles, reps, block, 2 * width), BF16),
        [pltpu.VMEM((width // LANES, block * tiles, LANES), F32)],
        (tile_ranks, source, *[bases[step] for step in range(1, reps)]),
    )
    adjoint, corr = call(
        functools.partial(final_kernel, tiles=tiles, reps=reps),
        "v" * (tiles + 2),
        [shaped((2, share, width), F32), shaped((2, share, points), F32)],
        [pltpu.VMEM((share, tiles * reps * block), BF16)],
        (own_corr, own_back, basis, *[sent[step] for step in range(1, tiles)]),
    )
    return forward_data, adjoint, corr


def bucket_live(rank_column, ranks):
    return (lax.iota(jnp.int32, ranks) // BUCKET)[:, None] < rank_column[None, :]


def long_path(focusing, source_basis, receiver_basis, tile_ranks, keep_counts):
    width = focusing.shape[2]
    share = focusing.shape[1] // lax.axis_size("rep")
    weights = (lax.iota(jnp.int32, width) < keep_counts[0]).astype(F32)
    factor = 1.0 / math.sqrt(SPAN * width * lax.axis_size("tile"))
    source = lax.all_gather(source_basis, "rep", axis=1, tiled=True)
    receiver = lax.all_gather(receiver_basis, "rep", axis=1, tiled=True)
    focal = lax.dynamic_slice_in_dim(focusing, lax.axis_index("rep") * share, share, 1)
    ranks, cells = source.shape[1], source.shape[2]
    live = bucket_live(tile_ranks[:, 0], ranks)

    blocks = dot(source.reshape(-1, width), focal.reshape(-1, width), NT)
    blocks = blocks.reshape(2, ranks, cells, 2, share)
    coef = jnp.stack([blocks[0, :, :, 0] - blocks[1, :, :, 1], blocks[0, :, :, 1] + blocks[1, :, :, 0]])
    coef = jnp.where(live[None, :, :, None], coef, 0.0).astype(BF16)[:, :, :, None]
    coef = lax.all_to_all(coef, "tile", split_axis=2, concat_axis=3, tiled=True)
    coef = coef.reshape(2, ranks * cells, share)
    flat = receiver.reshape(2, ranks * cells, width)
    blocks = jnp.einsum("wgh,lgj->wlhj", coef, flat, preferred_element_type=F32)
    forward_data = jnp.stack([blocks[0, 0] - blocks[1, 1], blocks[1, 0] + blocks[0, 1]])
    masked = (forward_data * weights).astype(BF16)

    blocks = jnp.einsum("pks,qfs->pqkf", flat, masked, preferred_element_type=F32)
    back = jnp.stack([blocks[0, 0] + blocks[1, 1], blocks[0, 1] - blocks[1, 0]]).astype(BF16)
    back = back.reshape(2, ranks, 1, cells, share)
    back = lax.all_to_all(back, "tile", split_axis=3, concat_axis=2, tiled=True)
    back = jnp.where(live[None, :, :, None, None], back, jnp.zeros((), BF16)).reshape(2, ranks * cells, share)
    flat = source.reshape(2, ranks * cells, width)
    blocks = jnp.einsum("wgh,lgj->wlhj", back, flat, preferred_element_type=F32)
    adjoint = jnp.stack([blocks[0, 0] + blocks[1, 1], blocks[1, 0] - blocks[0, 1]])
    blocks = jnp.einsum(
        "pgs,qfs->pqgf", adjoint, focusing.astype(F32), precision=lax.Precision.HIGHEST, preferred_element_type=F32
    )
    corr = factor * jnp.stack([blocks[0, 0] + blocks[1, 1], blocks[1, 0] - blocks[0, 1]])
    return forward_data, adjoint, lax.psum(corr, "tile")


def power_of_two(n):
    return n & (n - 1) == 0


def solution(mesh):
    tiles, reps = mesh.shape["tile"], mesh.shape["rep"]
    short = tiles <= 4 and power_of_two(tiles) and power_of_two(reps)

    def per_device(*args):
        return (short_path if short else long_path)(*args)

    placed = (
        P(None, "grp", "tile"),
        P(None, "rep", "grp", "tile"),
        P(None, "rep", "grp", "tile"),
        P("grp", "tile"),
        P(("grp", "tile")),
    )
    return jax.shard_map(
        per_device,
        mesh=mesh,
        in_specs=placed,
        out_specs=(P(None, ("grp", "rep"), "tile"), P(None, ("grp", "rep"), "tile"), P(None, "rep", "grp")),
        check_vma=False,
    )
```

time: 87.1 us -> 43.2 us (0.50)
  waiting for transfers between devices: 39.1 us -> 6.09 us
  between operations: 14.9 us -> 1.45 us
  blocking collectives: 13.3 us -> 0 us
  Pallas kernels: 0 us -> 10.6 us
  starting transfers between devices: 10.1 us -> 18.6 us
  other arithmetic: 1.89 us -> 0 us
  matrix products: 1.25 us -> 0 us
    psum x1 -> x0, waiting for transfers between devices: 33.4 us -> none  [per_device(): lax.psum(correlate(muted_adjoint_result, focusing, factor), 'tile')]
    ppermute x0 -> x15, starting transfers between devices: none -> 18.6 us  [swap(): return lax.ppermute(x, axis, [(i, i ^ step) for i in range(count)])]
    all_gather x2 -> x0, blocking collectives: 13.3 us -> none  [the longest x1 7.57 us: per_device(): lax.all_gather(source_basis, 'rep', axis=1, tiled=True)]
    pallas_call x0 -> x5, Pallas kernels: none -> 10.6 us  [call(): pl.pallas_call(kernel, in_specs=[smem if kind == 's' else vmem for kind i...]
    all_to_all x2 -> x0, starting transfers between devices: 10.1 us -> none  [the longest x1 5.09 us: adjoint_regroup(): lax.all_to_all(coefficient, 'tile', split_axis=3, concat_axis=2, tiled=True)]
    ppermute x0 -> x15, waiting for transfers between devices: none -> 6.09 us  [swap(): return lax.ppermute(x, axis, [(i, i ^ step) for i in range(count)])]
    all_to_all x2 -> x0, waiting for transfers between devices: 5.68 us -> none  [the longest x1 5.67 us: adjoint_regroup(): lax.all_to_all(coefficient, 'tile', split_axis=3, concat_axis=2, tiled=True)]
    dot_general x5 -> x0, matrix products: 1.25 us -> none  [the longest x1 0.4 us: correlate(): jnp.einsum('pgs,qfs->pqgf', image_part, focusing.astype(jnp.float32), pre...]
  transfers between devices with their start and end apart: 3 -> 15, of which waited for: 2 -> 2; matrix products, arithmetic and copies ran while one was open for 0% -> 5% of each run, Pallas kernels for 0% -> 20%
where the time goes in v1:
time: 43.2 us; the launch traced here: 42.9 us
  starting transfers between devices  18.6 us (43%)
  Pallas kernels  10.6 us (25%)
  local copies, waits for them, and re-layouts  6.12 us (14%)
  waiting for transfers between devices  6.09 us (14%)
  between operations  1.45 us (3%)
    ppermute x15, starting transfers between devices, swap(): return lax.ppermute(x, axis, [(i, i ^ step) for i in range(count)])  18.6 us
    pallas_call x5, Pallas kernels, call(): pl.pallas_call(kernel, in_specs=[smem if kind == 's' else vmem for kind i...  10.6 us
    ppermute x15, waiting for transfers between devices, swap(): return lax.ppermute(x, axis, [(i, i ^ step) for i in range(count)])  6.09 us
    unnamed x40, local copies, waits for them, and re-layouts  4.59 us
    reshape x1, local copies, waits for them, and re-layouts, short_path(): receiver = receiver_basis.reshape(2 * ranks * tiles, width)  0.89 us
  transfers between devices with their start and end apart: 15, of which 2 were waited for; matrix products, arithmetic and copies ran while one was open for 5% of the time, Pallas kernels for 20%

profile of v1, /device:TPU:0, one launch (start us, length us, event | category | flops | bytes accessed | tf_op | source)
XLA Modules:
  0.0 42.9 jit_solution(11797833529456319470)
XLA Ops:
  0.6 0.9 %reshape.17.refs_0_ = bf16[128,256]{1,0:T(8,128)(2,1)S(1)} reshape(bf16[2,16,4,256]{3,2,1,0:T(4,128)(2,1)} %param.7) | data formatting | bytes 131072 | tf_op jit(solution)/shard_map/reshape | solution.py:190
  2.1 2.6 %collective-permute-start.7 = (bf16[128,256]{1,0:T(8,128)(2,1)S(1)}, bf16[128,256]{1,0:T(8,128)(2,1)S(1)}, u32[]{:S(2)}, u32[]{:S(2)}) collective-permute-start(bf16[128,256]{1,0:T(8,128)(2,1)S(1)} %reshape.17.refs_0_), channel_id=1, source_target_pairs={{0,2},{1,3},{2,0},{3,1},{4,6},{5,7},{6,4},{7,5},{8,10},{9,11},{10,... | collective-permute-start | bytes 196616 | tf_op jit(solution)/shard_map/ppermute | solution.py:28
  4.7 0.6 %reshape.15.basis_ref.refs_0_ = bf16[128,256]{1,0:T(8,128)(2,1)} reshape(bf16[2,16,4,256]{3,2,1,0:T(4,128)(2,1)S(1)} %copy-done.12) | data formatting | bytes 131072 | tf_op jit(solution)/shard_map/reshape | solution.py:189
  5.4 0.7 %copy.8.ranks_ref = s32[4,1]{1,0:T(4,128)} copy(s32[4,1]{0,1:T(1,128)S(1)} %copy-done.16) | data formatting | bytes 32 | tf_op args[3]
  6.0 1.9 %shard_map.76 = (bf16[32,256]{1,0:T(8,128)(2,1)}, bf16[32,256]{1,0:T(8,128)(2,1)}, bf16[32,256]{1,0:T(8,128)(2,1)}, bf16[32,256]{1,0:T(8,128)(2,1)}) custom-call(s32[4,1]{1,0:T(4,128)} %copy.8.ranks_ref, bf16[128,256]{1,0:T(8,128)(2,1)} %reshape.15.basis_ref.refs_0_, bf16[512,256]{1,0:T(8,128)(2,1)} %bitcast.1), custom_call_target="tpu_custom_call" | custom-call | tf_op jit(solution)/shard_map/pallas_call | solution.py:169
  7.9 1.8 %collective-permute-start = (bf16[32,256]{1,0:T(8,128)(2,1)}, bf16[32,256]{1,0:T(8,128)(2,1)S(1)}, u32[]{:S(2)}, u32[]{:S(2)}) collective-permute-start(bf16[32,256]{1,0:T(8,128)(2,1)} %get-tuple-element.18), channel_id=1, source_target_pairs={{0,4},{4,0},{8,12},{12,8},{1,5},{5,1},{9,13},{13,9},{2,6},{6,2},{1... | collective-permute-start | bytes 49160 | tf_op jit(solution)/shard_map/ppermute | solution.py:28
  9.7 2.6 %collective-permute-start.1 = (bf16[32,256]{1,0:T(8,128)(2,1)}, bf16[32,256]{1,0:T(8,128)(2,1)S(1)}, u32[]{:S(2)}, u32[]{:S(2)}) collective-permute-start(bf16[32,256]{1,0:T(8,128)(2,1)} %get-tuple-element.19), channel_id=1, source_target_pairs={{0,8},{4,12},{8,0},{12,4},{1,9},{5,13},{9,1},{13,5},{2,10},{6,14},... | collective-permute-start | bytes 49160 | tf_op jit(solution)/shard_map/ppermute | solution.py:28
  12.3 0.8 %constant_dynamic-update-slice_fusion.3 = bf16[128,256]{1,0:T(8,128)(2,1)S(1)} fusion(bf16[32,256]{1,0:T(8,128)(2,1)} %get-tuple-element.17), kind=kLoop, calls=%fused_computation.3 | loop fusion | bytes 32768
  13.1 2.6 %collective-permute-start.2 = (bf16[32,256]{1,0:T(8,128)(2,1)S(1)}, bf16[32,256]{1,0:T(8,128)(2,1)S(1)}, u32[]{:S(2)}, u32[]{:S(2)}) collective-permute-start(bf16[32,256]{1,0:T(8,128)(2,1)S(1)} %copy-done.17), channel_id=1, source_target_pairs={{0,12},{4,8},{8,4},{12,0},{1,13},{5,9},{9,5},{13,1},{2,14},{6,10},... | collective-permute-start | bytes 49160 | tf_op jit(solution)/shard_map/ppermute | solution.py:28
  15.7 2.9 %collective-permute-done.2 = bf16[32,256]{1,0:T(8,128)(2,1)S(1)} collective-permute-done((bf16[32,256]{1,0:T(8,128)(2,1)S(1)}, bf16[32,256]{1,0:T(8,128)(2,1)S(1)}, u32[]{:S(2)}, u32[]{:S(2)}) %collective-permute-start.2) | collective-permute-done | bytes 16416 | tf_op jit(solution)/shard_map/ppermute | solution.py:28
  18.6 1.6 %collective-permute-start.4 = (bf16[128,256]{1,0:T(8,128)(2,1)S(1)}, bf16[128,256]{1,0:T(8,128)(2,1)S(1)}, u32[]{:S(2)}, u32[]{:S(2)}) collective-permute-start(bf16[128,256]{1,0:T(8,128)(2,1)S(1)} %constant_dynamic-update-slice_fusion.refs_0_), channel_id=1, source_target_pairs={{0,2},{1,3},{2,0},{3,1},{4,6},{5,7},{6,4},{7,5},{8,10},{9,11},{10,... | collective-permute-start | bytes 196616 | tf_op jit(solution)/shard_map/ppermute | solution.py:28
  20.5 1.6 %collective-permute-start.10 = (bf16[128,256]{1,0:T(8,128)(2,1)S(1)}, bf16[128,256]{1,0:T(8,128)(2,1)S(1)}, u32[]{:S(2)}, u32[]{:S(2)}) collective-permute-start(bf16[128,256]{1,0:T(8,128)(2,1)S(1)} %copy-done), channel_id=1, source_target_pairs={{0,2},{1,3},{2,0},{3,1},{4,6},{5,7},{6,4},{7,5},{8,10},{9,11},{10,... | collective-permute-start | bytes 196616 | tf_op jit(solution)/shard_map/ppermute | solution.py:28
  22.7 0.6 %copy-done.15 = bf16[128,256]{1,0:T(8,128)(2,1)} copy-done((bf16[128,256]{1,0:T(8,128)(2,1)}, bf16[128,256]{1,0:T(8,128)(2,1)S(1)}, u32[]{:S(2)}) %copy-start.15) | copy-done | bytes 65560
  23.3 1.8 %shard_map.77 = (bf16[4,4,32,512]{3,2,1,0:T(8,128)(2,1)}, f32[8,512]{1,0:T(8,128)}) custom-call(s32[1]{0:T(128)S(6)} %copy.13.keep_ref, bf16[128,256]{1,0:T(8,128)(2,1)} %copy-done.1, bf16[128,256]{1,0:T(8,128)(2,1)} %copy-done.13, bf16[128,256]{1,0:T(8,128)(2,1)} %copy-done.14, bf16[128,256]{1,0:T(8,128)(2,1)} %copy-done.15), custom_call_target="tpu_custom_call" | custom-call | tf_op jit(solution)/shard_map/pallas_call | solution.py:169
  25.8 3.0 %shard_map.78 = (f32[2,64,256]{2,1,0:T(8,128)}, f32[128,256]{1,0:T(8,128)}, bf16[64,128]{1,0:T(8,128)(2,1)}, bf16[160,256]{1,0:T(8,128)(2,1)}, bf16[160,256]{1,0:T(8,128)(2,1)}, /*index=5*/bf16[160,256]{1,0:T(8,128)(2,1)}) custom-call(bf16[128,256]{1,0:T(8,128)(2,1)} %copy-done.2, bf16[128,256]{1,0:T(8,128)(2,1)} %copy-done.7, bf16[128,256]{1,0:T(8,128)(2,1)} %copy-done.8, ...), custom_call_target="tpu_custom_call" | custom-call | tf_op jit(solution)/shard_map/pallas_call | solution.py:169
  28.8 3.2 %collective-permute-start.13 = (bf16[160,256]{1,0:T(8,128)(2,1)}, bf16[160,256]{1,0:T(8,128)(2,1)S(1)}, u32[]{:S(2)}, u32[]{:S(2)}) collective-permute-start(bf16[160,256]{1,0:T(8,128)(2,1)} %get-tuple-element.27), channel_id=1, source_target_pairs={{0,8},{4,12},{8,0},{12,4},{1,9},{5,13},{9,1},{13,5},{2,10},{6,14},... | collective-permute-start | bytes 245768 | tf_op jit(solution)/shard_map/ppermute | solution.py:28
  32.0 1.2 %collective-permute-start.14 = (bf16[160,256]{1,0:T(8,128)(2,1)}, bf16[160,256]{1,0:T(8,128)(2,1)S(1)}, u32[]{:S(2)}, u32[]{:S(2)}) collective-permute-start(bf16[160,256]{1,0:T(8,128)(2,1)} %get-tuple-element.28), channel_id=1, source_target_pairs={{0,12},{4,8},{8,4},{12,0},{1,13},{5,9},{9,5},{13,1},{2,14},{6,10},... | collective-permute-start | bytes 245768 | tf_op jit(solution)/shard_map/ppermute | solution.py:28
  33.2 0.6 %collective-permute-start.9 = (bf16[128,256]{1,0:T(8,128)(2,1)S(1)}, bf16[128,256]{1,0:T(8,128)(2,1)S(1)}, u32[]{:S(2)}, u32[]{:S(2)}) collective-permute-start(bf16[128,256]{1,0:T(8,128)(2,1)S(1)} %copy-done), channel_id=1, source_target_pairs={{0,1},{1,0},{2,3},{3,2},{4,5},{5,4},{6,7},{7,6},{8,9},{9,8},{10,11... | collective-permute-start | bytes 196616 | tf_op jit(solution)/shard_map/ppermute | solution.py:28
  33.9 3.2 %collective-permute-done.11.refs_3_ = bf16[128,256]{1,0:T(8,128)(2,1)S(1)} collective-permute-done((bf16[128,256]{1,0:T(8,128)(2,1)S(1)}, bf16[128,256]{1,0:T(8,128)(2,1)S(1)}, u32[]{:S(2)}, u32[]{:S(2)}) %collective-permute-start.11) | collective-permute-done | bytes 65568 | tf_op jit(solution)/shard_map/ppermute | solution.py:28
  37.0 0.6 %copy-done.10 = bf16[128,256]{1,0:T(8,128)(2,1)} copy-done((bf16[128,256]{1,0:T(8,128)(2,1)}, bf16[128,256]{1,0:T(8,128)(2,1)S(1)}, u32[]{:S(2)}) %copy-start.10) | copy-done | bytes 65560
  37.6 0.6 %copy-done.11 = bf16[128,256]{1,0:T(8,128)(2,1)} copy-done((bf16[128,256]{1,0:T(8,128)(2,1)}, bf16[128,256]{1,0:T(8,128)(2,1)S(1)}, u32[]{:S(2)}) %copy-start.11) | copy-done | bytes 65560
  38.3 1.8 %shard_map.79.refs_2_ = bf16[4,4,32,512]{3,2,1,0:T(8,128)(2,1)} custom-call(s32[4,1]{1,0:T(4,128)} %copy.8.ranks_ref, bf16[128,256]{1,0:T(8,128)(2,1)} %reshape.15.basis_ref.refs_0_, bf16[128,256]{1,0:T(8,128)(2,1)} %copy-done.11, bf16[128,256]{1,0:T(8,128)(2,1)} %copy-done.6, bf16[128,256]{1,0:T(8,128)(2,1)} %copy-done.10), custom_call_target="tpu_custom_call" | custom-call | tf_op jit(solution)/shard_map/pallas_call | solution.py:169
  40.1 0.6 %copy-done.3 = bf16[160,256]{1,0:T(8,128)(2,1)} copy-done((bf16[160,256]{1,0:T(8,128)(2,1)}, bf16[160,256]{1,0:T(8,128)(2,1)S(1)}, u32[]{:S(2)}) %copy-start.3) | copy-done | bytes 81944
  40.8 2.1 %shard_map.80 = (f32[2,64,256]{2,1,0:T(8,128)}, f32[2,64,256]{2,1,0:T(8,128)}) custom-call(f32[128,256]{1,0:T(8,128)} %get-tuple-element.24.refs_0_, bf16[64,128]{1,0:T(8,128)(2,1)} %get-tuple-element.25.refs_1_, bf16[4,4,32,512]{3,2,1,0:T(8,128)(2,1)} %shard_map.79.refs_2_, bf16[160,256]{1,0:T(8,128)(2,1)} %copy-done.3, bf16[160,256]{1,0:T(8,128)(2,1)} %copy-done.4, ...), custom_call_target="tpu_custom_call" | custom-call | tf_op jit(solution)/shard_map/pallas_call | solution.py:169
  (54 shorter events, 1.7 us)
Async XLA Ops:
  0.6 4.1 %copy-start.12 = (bf16[2,16,4,256]{3,2,1,0:T(4,128)(2,1)S(1)}, bf16[2,16,4,256]{3,2,1,0:T(4,128)(2,1)}, u32[]{:S(2)}) copy-start(bf16[2,16,4,256]{3,2,1,0:T(4,128)(2,1)} %param.6) | copy-start | bytes 196612
  1.5 3.8 %copy-start.1 = (bf16[128,256]{1,0:T(8,128)(2,1)}, bf16[128,256]{1,0:T(8,128)(2,1)S(1)}, u32[]{:S(2)}) copy-start(bf16[128,256]{1,0:T(8,128)(2,1)S(1)} %reshape.17.refs_0_) | copy-start | bytes 196612
  1.5 3.8 %copy-start.16 = (s32[4,1]{0,1:T(1,128)S(1)}, s32[4,1]{0,1:T(1,128)}, u32[]{:S(2)}) copy-start(s32[4,1]{0,1:T(1,128)} %param.8) | copy-start | bytes 52
  1.6 18.6 %collective-permute-start.6 = (bf16[128,256]{1,0:T(8,128)(2,1)S(1)}, bf16[128,256]{1,0:T(8,128)(2,1)S(1)}, u32[]{:S(2)}, u32[]{:S(2)}) collective-permute-start(bf16[128,256]{1,0:T(8,128)(2,1)S(1)} %reshape.17.refs_0_), channel_id=1, source_target_pairs={{0,1},{1,0},{2,3},{3,2},{4,5},{5,4},{6,7},{7,6},{8,9},{9,8},{10,11... | collective-permute-start | bytes 196616 | tf_op jit(solution)/shard_map/ppermute | solution.py:28
  2.1 18.4 %collective-permute-start.7 = (bf16[128,256]{1,0:T(8,128)(2,1)S(1)}, bf16[128,256]{1,0:T(8,128)(2,1)S(1)}, u32[]{:S(2)}, u32[]{:S(2)}) collective-permute-start(bf16[128,256]{1,0:T(8,128)(2,1)S(1)} %reshape.17.refs_0_), channel_id=1, source_target_pairs={{0,2},{1,3},{2,0},{3,1},{4,6},{5,7},{6,4},{7,5},{8,10},{9,11},{10,... | collective-permute-start | bytes 196616 | tf_op jit(solution)/shard_map/ppermute | solution.py:28
  4.7 18.0 %collective-permute-start.8 = (bf16[128,256]{1,0:T(8,128)(2,1)S(1)}, bf16[128,256]{1,0:T(8,128)(2,1)S(1)}, u32[]{:S(2)}, u32[]{:S(2)}) collective-permute-start(bf16[128,256]{1,0:T(8,128)(2,1)S(1)} %reshape.17.refs_0_), channel_id=1, source_target_pairs={{0,3},{1,2},{2,1},{3,0},{4,7},{5,6},{6,5},{7,4},{8,11},{9,10},{10,... | collective-permute-start | bytes 196616 | tf_op jit(solution)/shard_map/ppermute | solution.py:28
  7.9 5.2 %collective-permute-start = (bf16[32,256]{1,0:T(8,128)(2,1)}, bf16[32,256]{1,0:T(8,128)(2,1)S(1)}, u32[]{:S(2)}, u32[]{:S(2)}) collective-permute-start(bf16[32,256]{1,0:T(8,128)(2,1)} %get-tuple-element.18), channel_id=1, source_target_pairs={{0,4},{4,0},{8,12},{12,8},{1,5},{5,1},{9,13},{13,9},{2,6},{6,2},{1... | collective-permute-start | bytes 49160 | tf_op jit(solution)/shard_map/ppermute | solution.py:28
  9.7 6.0 %collective-permute-start.1 = (bf16[32,256]{1,0:T(8,128)(2,1)}, bf16[32,256]{1,0:T(8,128)(2,1)S(1)}, u32[]{:S(2)}, u32[]{:S(2)}) collective-permute-start(bf16[32,256]{1,0:T(8,128)(2,1)} %get-tuple-element.19), channel_id=1, source_target_pairs={{0,8},{4,12},{8,0},{12,4},{1,9},{5,13},{9,1},{13,5},{2,10},{6,14},... | collective-permute-start | bytes 49160 | tf_op jit(solution)/shard_map/ppermute | solution.py:28
  12.3 0.8 %copy-start.17 = (bf16[32,256]{1,0:T(8,128)(2,1)S(1)}, bf16[32,256]{1,0:T(8,128)(2,1)}, u32[]{:S(2)}) copy-start(bf16[32,256]{1,0:T(8,128)(2,1)} %get-tuple-element.20) | copy-start | bytes 49156
  12.3 8.2 %copy-start = (bf16[128,256]{1,0:T(8,128)(2,1)S(1)}, bf16[128,256]{1,0:T(8,128)(2,1)}, u32[]{:S(2)}) copy-start(bf16[128,256]{1,0:T(8,128)(2,1)} %reshape.15.basis_ref.refs_0_) | copy-start | bytes 196612
  13.1 5.5 %collective-permute-start.2 = (bf16[32,256]{1,0:T(8,128)(2,1)S(1)}, bf16[32,256]{1,0:T(8,128)(2,1)S(1)}, u32[]{:S(2)}, u32[]{:S(2)}) collective-permute-start(bf16[32,256]{1,0:T(8,128)(2,1)S(1)} %copy-done.17), channel_id=1, source_target_pairs={{0,12},{4,8},{8,4},{12,0},{1,13},{5,9},{9,5},{13,1},{2,14},{6,10},... | collective-permute-start | bytes 49160 | tf_op jit(solution)/shard_map/ppermute | solution.py:28
  18.6 6.6 %copy-start.2 = (bf16[128,256]{1,0:T(8,128)(2,1)}, bf16[128,256]{1,0:T(8,128)(2,1)S(1)}, u32[]{:S(2)}) copy-start(bf16[128,256]{1,0:T(8,128)(2,1)S(1)} %constant_dynamic-update-slice_fusion.refs_0_) | copy-start | bytes 196612
  18.6 6.6 %collective-permute-start.3 = (bf16[128,256]{1,0:T(8,128)(2,1)S(1)}, bf16[128,256]{1,0:T(8,128)(2,1)S(1)}, u32[]{:S(2)}, u32[]{:S(2)}) collective-permute-start(bf16[128,256]{1,0:T(8,128)(2,1)S(1)} %constant_dynamic-update-slice_fusion.refs_0_), channel_id=1, source_target_pairs={{0,1},{1,0},{2,3},{3,2},{4,5},{5,4},{6,7},{7,6},{8,9},{9,8},{10,11... | collective-permute-start | bytes 196616 | tf_op jit(solution)/shard_map/ppermute | solution.py:28
  18.6 6.6 %collective-permute-start.4 = (bf16[128,256]{1,0:T(8,128)(2,1)S(1)}, bf16[128,256]{1,0:T(8,128)(2,1)S(1)}, u32[]{:S(2)}, u32[]{:S(2)}) collective-permute-start(bf16[128,256]{1,0:T(8,128)(2,1)S(1)} %constant_dynamic-update-slice_fusion.refs_0_), channel_id=1, source_target_pairs={{0,2},{1,3},{2,0},{3,1},{4,6},{5,7},{6,4},{7,5},{8,10},{9,11},{10,... | collective-permute-start | bytes 196616 | tf_op jit(solution)/shard_map/ppermute | solution.py:28
  20.2 2.5 %copy-start.13 = (bf16[128,256]{1,0:T(8,128)(2,1)}, bf16[128,256]{1,0:T(8,128)(2,1)S(1)}, u32[]{:S(2)}) copy-start(bf16[128,256]{1,0:T(8,128)(2,1)S(1)} %collective-permute-done.6.refs_1_) | copy-start | bytes 196612
  20.2 5.0 %collective-permute-start.5 = (bf16[128,256]{1,0:T(8,128)(2,1)S(1)}, bf16[128,256]{1,0:T(8,128)(2,1)S(1)}, u32[]{:S(2)}, u32[]{:S(2)}) collective-permute-start(bf16[128,256]{1,0:T(8,128)(2,1)S(1)} %constant_dynamic-update-slice_fusion.refs_0_), channel_id=1, source_target_pairs={{0,3},{1,2},{2,1},{3,0},{4,7},{5,6},{6,5},{7,4},{8,11},{9,10},{10,... | collective-permute-start | bytes 196616 | tf_op jit(solution)/shard_map/ppermute | solution.py:28
  20.5 2.2 %copy-start.14 = (bf16[128,256]{1,0:T(8,128)(2,1)}, bf16[128,256]{1,0:T(8,128)(2,1)S(1)}, u32[]{:S(2)}) copy-start(bf16[128,256]{1,0:T(8,128)(2,1)S(1)} %collective-permute-done.7.refs_2_) | copy-start | bytes 196612
  20.5 12.7 %collective-permute-start.10 = (bf16[128,256]{1,0:T(8,128)(2,1)S(1)}, bf16[128,256]{1,0:T(8,128)(2,1)S(1)}, u32[]{:S(2)}, u32[]{:S(2)}) collective-permute-start(bf16[128,256]{1,0:T(8,128)(2,1)S(1)} %copy-done), channel_id=1, source_target_pairs={{0,2},{1,3},{2,0},{3,1},{4,6},{5,7},{6,4},{7,5},{8,10},{9,11},{10,... | collective-permute-start | bytes 196616 | tf_op jit(solution)/shard_map/ppermute | solution.py:28
  28.8 11.3 %collective-permute-start.12 = (bf16[160,256]{1,0:T(8,128)(2,1)}, bf16[160,256]{1,0:T(8,128)(2,1)S(1)}, u32[]{:S(2)}, u32[]{:S(2)}) collective-permute-start(bf16[160,256]{1,0:T(8,128)(2,1)} %get-tuple-element.26), channel_id=1, source_target_pairs={{0,4},{4,0},{8,12},{12,8},{1,5},{5,1},{9,13},{13,9},{2,6},{6,2},{1... | collective-permute-start | bytes 245768 | tf_op jit(solution)/shard_map/ppermute | solution.py:28
  28.8 11.3 %collective-permute-start.13 = (bf16[160,256]{1,0:T(8,128)(2,1)}, bf16[160,256]{1,0:T(8,128)(2,1)S(1)}, u32[]{:S(2)}, u32[]{:S(2)}) collective-permute-start(bf16[160,256]{1,0:T(8,128)(2,1)} %get-tuple-element.27), channel_id=1, source_target_pairs={{0,8},{4,12},{8,0},{12,4},{1,9},{5,13},{9,1},{13,5},{2,10},{6,14},... | collective-permute-start | bytes 245768 | tf_op jit(solution)/shard_map/ppermute | solution.py:28
  32.0 8.1 %collective-permute-start.14 = (bf16[160,256]{1,0:T(8,128)(2,1)}, bf16[160,256]{1,0:T(8,128)(2,1)S(1)}, u32[]{:S(2)}, u32[]{:S(2)}) collective-permute-start(bf16[160,256]{1,0:T(8,128)(2,1)} %get-tuple-element.28), channel_id=1, source_target_pairs={{0,12},{4,8},{8,4},{12,0},{1,13},{5,9},{9,5},{13,1},{2,14},{6,10},... | collective-permute-start | bytes 245768 | tf_op jit(solution)/shard_map/ppermute | solution.py:28
  33.2 3.8 %collective-permute-start.11 = (bf16[128,256]{1,0:T(8,128)(2,1)S(1)}, bf16[128,256]{1,0:T(8,128)(2,1)S(1)}, u32[]{:S(2)}, u32[]{:S(2)}) collective-permute-start(bf16[128,256]{1,0:T(8,128)(2,1)S(1)} %copy-done), channel_id=1, source_target_pairs={{0,3},{1,2},{2,1},{3,0},{4,7},{5,6},{6,5},{7,4},{8,11},{9,10},{10,... | collective-permute-start | bytes 196616 | tf_op jit(solution)/shard_map/ppermute | solution.py:28
  33.2 3.8 %copy-start.6 = (bf16[128,256]{1,0:T(8,128)(2,1)}, bf16[128,256]{1,0:T(8,128)(2,1)S(1)}, u32[]{:S(2)}) copy-start(bf16[128,256]{1,0:T(8,128)(2,1)S(1)} %collective-permute-done.10.refs_2_) | copy-start | bytes 196612
  33.2 3.8 %collective-permute-start.9 = (bf16[128,256]{1,0:T(8,128)(2,1)S(1)}, bf16[128,256]{1,0:T(8,128)(2,1)S(1)}, u32[]{:S(2)}, u32[]{:S(2)}) collective-permute-start(bf16[128,256]{1,0:T(8,128)(2,1)S(1)} %copy-done), channel_id=1, source_target_pairs={{0,1},{1,0},{2,3},{3,2},{4,5},{5,4},{6,7},{7,6},{8,9},{9,8},{10,11... | collective-permute-start | bytes 196616 | tf_op jit(solution)/shard_map/ppermute | solution.py:28
  (9 other events, 5.7 us)

commit v2 on v1

--- a/solution.py
+++ b/solution.py
@@ -28,75 +28,58 @@
     return lax.ppermute(x, axis, [(i, i ^ step) for i in range(count)])
 
 
-LANES = 128
-
-
-def fold(ref, start, value):
-    rows, columns = value.shape
-    for part in range(columns // LANES):
-        ref[part, pl.ds(start, rows), :] = value[:, part * LANES : (part + 1) * LANES]
-
-
-def every(ref, start, count, stride):
-    parts = [ref[part, pl.ds(start, count, stride=stride), :] for part in range(ref.shape[0])]
-    return jnp.concatenate(parts, axis=1)
-
-
 def live_rows(ranks_ref, cell, shard, ranks):
     rows = lax.broadcasted_iota(jnp.int32, (ranks, 1), 0) + shard * ranks
-    return rows < ranks_ref[cell, 0] * BUCKET
-
-
-def forward_kernel(ranks_ref, basis_ref, foc_ref, *refs, tiles, ranks):
-    outs, made, blocks = refs[:tiles], refs[tiles], refs[tiles + 1]
+    return rows < ranks_ref[cell] * BUCKET
+
+
+def forward_kernel(ranks_ref, basis_ref, foc_ref, *refs):
+    ranks, tiles = basis_ref.shape[1], basis_ref.shape[2]
+    outs, blocks = refs[:tiles], refs[tiles]
     here = lax.axis_index("tile")
     shard = lax.axis_index("rep")
-    half = ranks * tiles
     points = foc_ref.shape[0] // 2
-    prod = dot(basis_ref[...], foc_ref[...], NT)
-    fold(made, 0, prod[:half, :points] - prod[half:, points:])
-    fold(made, half, prod[:half, points:] + prod[half:, :points])
+    rows = [basis_ref[part, :, cell, :] for cell in range(tiles) for part in range(2)]
+    prod = dot(jnp.concatenate(rows, axis=0), foc_ref[...], NT)
     for cell in range(tiles):
         mask = live_rows(ranks_ref, cell, shard, ranks)
+        real = prod[2 * cell * ranks : (2 * cell + 1) * ranks]
+        imag = prod[(2 * cell + 1) * ranks : (2 * cell + 2) * ranks]
+        coef = [real[:, :points] - imag[:, points:], real[:, points:] + imag[:, :points]]
         for part in range(2):
-            rows = every(made, part * half + cell, ranks, tiles)
-            blocks[cell, pl.ds(part * ranks, ranks), :] = jnp.where(mask, rows, 0.0).astype(BF16)
+            blocks[cell, pl.ds(part * ranks, ranks), :] = jnp.where(mask, coef[part], 0.0).astype(BF16)
     for step in range(tiles):
         outs[step][...] = blocks[here ^ step]
 
 
-def lift_kernel(keep_ref, *refs, tiles, reps, ranks):
-    pieces, out, weight, wide = refs[:reps], refs[reps], refs[reps + 1], refs[reps + 2]
+def lift_kernel(keep_ref, *refs, reps):
+    pieces, out, weight = refs[:reps], refs[reps], refs[reps + 1]
+    ranks, tiles, width = pieces[0].shape[1:]
     here = lax.axis_index("tile")
-    half = ranks * tiles
-    width = pieces[0].shape[1]
     columns = lax.broadcasted_iota(jnp.int32, weight.shape, 1)
     columns = jnp.where(columns >= width, columns - width, columns)
     weight[...] = (columns < keep_ref[0]).astype(F32)
     for shard in range(reps):
-        fold(wide, 0, pieces[shard][...].astype(F32))
         for cell in range(tiles):
-            real = every(wide, cell, ranks, tiles)
-            imag = every(wide, half + cell, ranks, tiles)
+            real = pieces[shard][0, :, cell, :]
+            imag = pieces[shard][1, :, cell, :]
             spot = here ^ cell
-            out[spot, shard, pl.ds(0, ranks), pl.ds(0, width)] = real.astype(BF16)
-            out[spot, shard, pl.ds(0, ranks), pl.ds(width, width)] = imag.astype(BF16)
-            out[spot, shard, pl.ds(ranks, ranks), pl.ds(0, width)] = (-imag).astype(BF16)
-            out[spot, shard, pl.ds(ranks, ranks), pl.ds(width, width)] = real.astype(BF16)
-
-
-def image_basis_kernel(ranks_ref, *refs, tiles, reps, ranks):
-    pieces, out, wide = refs[:reps], refs[reps], refs[reps + 1]
+            out[spot, shard, pl.ds(0, ranks), pl.ds(0, width)] = real
+            out[spot, shard, pl.ds(0, ranks), pl.ds(width, width)] = imag
+            out[spot, shard, pl.ds(ranks, ranks), pl.ds(0, width)] = -imag
+            out[spot, shard, pl.ds(ranks, ranks), pl.ds(width, width)] = real
+
+
+def image_basis_kernel(ranks_ref, *refs, reps):
+    pieces, out = refs[:reps], refs[reps]
+    ranks, tiles, width = pieces[0].shape[1:]
     here = lax.axis_index("tile")
     me = lax.axis_index("rep")
-    half = ranks * tiles
-    width = pieces[0].shape[1]
     for shard in range(reps):
-        fold(wide, 0, pieces[shard][...].astype(F32))
         for cell in range(tiles):
             mask = live_rows(ranks_ref, cell, me ^ shard, ranks)
-            real = jnp.where(mask, every(wide, cell, ranks, tiles), 0.0)
-            imag = jnp.where(mask, every(wide, half + cell, ranks, tiles), 0.0)
+            real = jnp.where(mask, pieces[shard][0, :, cell, :].astype(F32), 0.0)
+            imag = jnp.where(mask, pieces[shard][1, :, cell, :].astype(F32), 0.0)
             spot = here ^ cell
             out[spot, shard, pl.ds(0, ranks), pl.ds(0, width)] = real.astype(BF16)
             out[spot, shard, pl.ds(0, ranks), pl.ds(width, width)] = (-imag).astype(BF16)
@@ -166,67 +149,67 @@
 
 def call(kernel, ins, outs, scratch, args):
     vmem, smem = pl.BlockSpec(memory_space=pltpu.VMEM), pl.BlockSpec(memory_space=pltpu.SMEM)
+    args = [pltpu.with_memory_space_constraint(a, pltpu.VMEM) if k == "p" else a for k, a in zip(ins, args)]
     return pl.pallas_call(
         kernel,
         in_specs=[smem if kind == "s" else vmem for kind in ins],
-        out_specs=jax.tree.map(lambda _: vmem, outs),
+        out_specs=[vmem] * len(outs),
         out_shape=outs,
         scratch_shapes=scratch,
     )(*args)
 
 
-def short_path(focusing, source_basis, receiver_basis, tile_ranks, keep_counts):
+def short_path(focusing, source, receiver, tile_ranks, keep_counts):
     tiles, reps = lax.axis_size("tile"), lax.axis_size("rep")
-    ranks, width = source_basis.shape[1], source_basis.shape[3]
+    ranks, width = source.shape[1], source.shape[3]
     points = focusing.shape[1]
     share = points // reps
     block = 2 * ranks
     factor = 1.0 / math.sqrt(SPAN * width * tiles)
-    shaped = jax.ShapeDtypeStruct
+    shaped, placed = jax.ShapeDtypeStruct, pltpu.VMEM
     order = sorted(range(1, tiles), reverse=True)
     rep_order = sorted(range(1, reps), key=lambda s: (s == 1, s))
-
-    source = source_basis.reshape(2 * ranks * tiles, width)
-    receiver = receiver_basis.reshape(2 * ranks * tiles, width)
+    live = tile_ranks.reshape(tiles)
+
     made = call(
-        functools.partial(forward_kernel, tiles=tiles, ranks=ranks),
+        forward_kernel,
         "svv",
-        [shaped((block, points), BF16)] * tiles,
-        [pltpu.VMEM((points // LANES, block * tiles, LANES), F32), pltpu.VMEM((tiles, block, points), BF16)],
-        (tile_ranks, source, focusing.reshape(2 * points, width)),
+        [placed((block, points), BF16)] * tiles,
+        [pltpu.VMEM((tiles, block, points), BF16)],
+        (live, source, focusing.reshape(2 * points, width)),
     )
     got = {step: swap(made[step], "tile", step) for step in order}
     lifts = {step: swap(receiver, "rep", step) for step in rep_order}
     gathered = jnp.concatenate([made[0]] + [got[step] for step in range(1, tiles)], axis=0)
     spread = {step: swap(gathered, "rep", step) for step in rep_order}
+    bases = {step: swap(source, "rep", step) for step in rep_order}
     lift, weight = call(
-        functools.partial(lift_kernel, tiles=tiles, reps=reps, ranks=ranks),
-        "s" + "v" * reps,
-        [shaped((tiles, reps, block, 2 * width), BF16), shaped((8, 2 * width), F32)],
-        [pltpu.VMEM((width // LANES, block * tiles, LANES), F32)],
+        functools.partial(lift_kernel, reps=reps),
+        "s" + "p" * reps,
+        [placed((tiles, reps, block, 2 * width), BF16), placed((8, 2 * width), F32)],
+        [],
         (keep_counts, receiver, *[lifts[step] for step in range(1, reps)]),
     )
     middle = call(
         functools.partial(middle_kernel, tiles=tiles, reps=reps, factor=factor),
-        "v" * (reps + 2),
-        [shaped((2, share, width), F32), shaped((2 * share, points), F32), shaped((share, reps * block), BF16)]
-        + [shaped((2 * share + share // 2, points), BF16)] * (tiles - 1),
+        "p" * (reps + 2),
+        [placed((2, share, width), F32), placed((2 * share, points), F32), placed((share, reps * block), BF16)]
+        + [placed((2 * share + share // 2, points), BF16)] * (tiles - 1),
         [pltpu.VMEM((points, 2 * width), F32)],
         (gathered, *[spread[step] for step in range(1, reps)], lift, weight),
     )
     forward_data, own_corr, own_back = middle[:3]
     sent = {step: swap(middle[2 + step], "tile", step) for step in order}
-    bases = {step: swap(source, "rep", step) for step in rep_order}
-    basis = call(
-        functools.partial(image_basis_kernel, tiles=tiles, reps=reps, ranks=ranks),
-        "s" + "v" * reps,
-        shaped((tiles, reps, block, 2 * width), BF16),
-        [pltpu.VMEM((width // LANES, block * tiles, LANES), F32)],
-        (tile_ranks, source, *[bases[step] for step in range(1, reps)]),
+    (basis,) = call(
+        functools.partial(image_basis_kernel, reps=reps),
+        "s" + "p" * reps,
+        [placed((tiles, reps, block, 2 * width), BF16)],
+        [],
+        (live, source, *[bases[step] for step in range(1, reps)]),
     )
     adjoint, corr = call(
         functools.partial(final_kernel, tiles=tiles, reps=reps),
-        "v" * (tiles + 2),
+        "p" * (tiles + 2),
         [shaped((2, share, width), F32), shaped((2, share, points), F32)],
         [pltpu.VMEM((share, tiles * reps * block), BF16)],
         (own_corr, own_back, basis, *[sent[step] for step in range(1, tiles)]),

time: 43.2 us -> 33.4 us (0.77)
  Pallas kernels: 10.6 us -> 4.81 us
  local copies, waits for them, and re-layouts: 6.12 us -> 0.67 us
  starting transfers between devices: 18.6 us -> 20.1 us
    pallas_call x5, Pallas kernels: 10.6 us -> 4.81 us  [call(): pl.pallas_call(kernel, in_specs=[smem if kind == 's' else vmem for kind i...]
    unnamed x40 -> x8, local copies, waits for them, and re-layouts: 4.59 us -> 0.67 us
    reshape x2 -> x0, local copies, waits for them, and re-layouts: 1.53 us -> none  [the longest x1 0.89 us: short_path(): receiver = receiver_basis.reshape(2 * ranks * tiles, width)]
    ppermute x15, starting transfers between devices: 18.6 us -> 20.1 us  [swap(): return lax.ppermute(x, axis, [(i, i ^ step) for i in range(count)])]
  transfers between devices with their start and end apart: 15 -> 15, of which waited for: 2 -> 4; matrix products, arithmetic and copies ran while one was open for 5% -> 2% of each run, Pallas kernels for 20% -> 12%
where the time goes in v2:
time: 33.4 us; the launch traced here: 33.2 us
  starting transfers between devices  20.1 us (60%)
  waiting for transfers between devices  6.21 us (19%)
  Pallas kernels  4.81 us (14%)
  between operations  1.37 us (4%)
  local copies, waits for them, and re-layouts  0.67 us (2%)
    ppermute x15, starting transfers between devices, swap(): return lax.ppermute(x, axis, [(i, i ^ step) for i in range(count)])  20.1 us
    ppermute x15, waiting for transfers between devices, swap(): return lax.ppermute(x, axis, [(i, i ^ step) for i in range(count)])  6.21 us
    pallas_call x5, Pallas kernels, call(): pl.pallas_call(kernel, in_specs=[smem if kind == 's' else vmem for kind i...  4.81 us
    unnamed x8, local copies, waits for them, and re-layouts  0.67 us
  transfers between devices with their start and end apart: 15, of which 4 were waited for; matrix products, arithmetic and copies ran while one was open for 2% of the time, Pallas kernels for 12%

profile of v2, /device:TPU:0, one launch (start us, length us, event | category | flops | bytes accessed | tf_op | source)
XLA Modules:
  0.0 33.2 jit_solution(500587267094830284)
XLA Ops:
  0.6 0.6 %collective-permute-start.6 = (bf16[2,16,4,256]{3,2,1,0:T(4,128)(2,1)}, bf16[2,16,4,256]{3,2,1,0:T(4,128)(2,1)S(1)}, u32[]{:S(2)}, u32[]{:S(2)}) collective-permute-start(bf16[2,16,4,256]{3,2,1,0:T(4,128)(2,1)} %refs_0_.2), channel_id=1, source_target_pairs={{0,1},{1,0},{2,3},{3,2},{4,5},{5,4},{6,7},{7,6},{8,9},{9,8},{10,11... | collective-permute-start | bytes 196616 | tf_op jit(solution)/shard_map/ppermute | solution.py:28
  1.2 2.6 %collective-permute-start.7 = (bf16[2,16,4,256]{3,2,1,0:T(4,128)(2,1)}, bf16[2,16,4,256]{3,2,1,0:T(4,128)(2,1)S(1)}, u32[]{:S(2)}, u32[]{:S(2)}) collective-permute-start(bf16[2,16,4,256]{3,2,1,0:T(4,128)(2,1)} %refs_0_.2), channel_id=1, source_target_pairs={{0,2},{1,3},{2,0},{3,1},{4,6},{5,7},{6,4},{7,5},{8,10},{9,11},{10,... | collective-permute-start | bytes 196616 | tf_op jit(solution)/shard_map/ppermute | solution.py:28
  3.7 0.0 collective-permute-start.8
  3.8 1.3 %shard_map.76 = (bf16[32,256]{1,0:T(8,128)(2,1)S(1)}, bf16[32,256]{1,0:T(8,128)(2,1)S(1)}, bf16[32,256]{1,0:T(8,128)(2,1)S(1)}, bf16[32,256]{1,0:T(8,128)(2,1)S(1)}) custom-call(s32[4]{0:T(128)} %bitcast.3, bf16[2,16,4,256]{3,2,1,0:T(4,128)(2,1)} %refs_0_.3, bf16[512,256]{1,0:T(8,128)(2,1)} %bitcast.2), custom_call_target="tpu_custom_call" | custom-call | tf_op jit(solution)/shard_map/pallas_call | solution.py:153
  5.1 1.9 %collective-permute-start = (bf16[32,256]{1,0:T(8,128)(2,1)S(1)}, bf16[32,256]{1,0:T(8,128)(2,1)S(1)}, u32[]{:S(2)}, u32[]{:S(2)}) collective-permute-start(bf16[32,256]{1,0:T(8,128)(2,1)S(1)} %get-tuple-element.18), channel_id=1, source_target_pairs={{0,4},{4,0},{8,12},{12,8},{1,5},{5,1},{9,13},{13,9},{2,6},{6,2},{1... | collective-permute-start | bytes 49160 | tf_op jit(solution)/shard_map/ppermute | solution.py:28
  6.9 2.6 %collective-permute-start.1 = (bf16[32,256]{1,0:T(8,128)(2,1)S(1)}, bf16[32,256]{1,0:T(8,128)(2,1)S(1)}, u32[]{:S(2)}, u32[]{:S(2)}) collective-permute-start(bf16[32,256]{1,0:T(8,128)(2,1)S(1)} %get-tuple-element.19), channel_id=1, source_target_pairs={{0,8},{4,12},{8,0},{12,4},{1,9},{5,13},{9,1},{13,5},{2,10},{6,14},... | collective-permute-start | bytes 49160 | tf_op jit(solution)/shard_map/ppermute | solution.py:28
  9.5 3.2 %collective-permute-start.2 = (bf16[32,256]{1,0:T(8,128)(2,1)S(1)}, bf16[32,256]{1,0:T(8,128)(2,1)S(1)}, u32[]{:S(2)}, u32[]{:S(2)}) collective-permute-start(bf16[32,256]{1,0:T(8,128)(2,1)S(1)} %get-tuple-element.20), channel_id=1, source_target_pairs={{0,12},{4,8},{8,4},{12,0},{1,13},{5,9},{9,5},{13,1},{2,14},{6,10},... | collective-permute-start | bytes 49160 | tf_op jit(solution)/shard_map/ppermute | solution.py:28
  12.7 2.4 %collective-permute-done.2 = bf16[32,256]{1,0:T(8,128)(2,1)S(1)} collective-permute-done((bf16[32,256]{1,0:T(8,128)(2,1)S(1)}, bf16[32,256]{1,0:T(8,128)(2,1)S(1)}, u32[]{:S(2)}, u32[]{:S(2)}) %collective-permute-start.2) | collective-permute-done | bytes 16416 | tf_op jit(solution)/shard_map/ppermute | solution.py:28
  15.2 1.5 %collective-permute-start.4 = (bf16[128,256]{1,0:T(8,128)(2,1)S(1)}, bf16[128,256]{1,0:T(8,128)(2,1)S(1)}, u32[]{:S(2)}, u32[]{:S(2)}) collective-permute-start(bf16[128,256]{1,0:T(8,128)(2,1)S(1)} %constant_dynamic-update-slice_fusion.refs_0_), channel_id=1, source_target_pairs={{0,2},{1,3},{2,0},{3,1},{4,6},{5,7},{6,4},{7,5},{8,10},{9,11},{10,... | collective-permute-start | bytes 196616 | tf_op jit(solution)/shard_map/ppermute | solution.py:28
  16.7 0.4 %collective-permute-start.5 = (bf16[128,256]{1,0:T(8,128)(2,1)S(1)}, bf16[128,256]{1,0:T(8,128)(2,1)S(1)}, u32[]{:S(2)}, u32[]{:S(2)}) collective-permute-start(bf16[128,256]{1,0:T(8,128)(2,1)S(1)} %constant_dynamic-update-slice_fusion.refs_0_), channel_id=1, source_target_pairs={{0,3},{1,2},{2,1},{3,0},{4,7},{5,6},{6,5},{7,4},{8,11},{9,10},{10,... | collective-permute-start | bytes 196616 | tf_op jit(solution)/shard_map/ppermute | solution.py:28
  17.0 1.5 %collective-permute-start.10 = (bf16[2,16,4,256]{3,2,1,0:T(4,128)(2,1)S(1)}, bf16[2,16,4,256]{3,2,1,0:T(4,128)(2,1)S(1)}, u32[]{:S(2)}, u32[]{:S(2)}) collective-permute-start(bf16[2,16,4,256]{3,2,1,0:T(4,128)(2,1)S(1)} %copy-done), channel_id=1, source_target_pairs={{0,2},{1,3},{2,0},{3,1},{4,6},{5,7},{6,4},{7,5},{8,10},{9,11},{10,... | collective-permute-start | bytes 196616 | tf_op jit(solution)/shard_map/ppermute | solution.py:28
  19.2 0.7 %shard_map.77 = (bf16[4,4,32,512]{3,2,1,0:T(8,128)(2,1)S(1)}, f32[8,512]{1,0:T(8,128)S(1)}) custom-call(s32[1]{0:T(128)S(6)} %copy.12.keep_ref, bf16[2,16,4,256]{3,2,1,0:T(4,128)(2,1)S(1)} %copy-done.1, bf16[2,16,4,256]{3,2,1,0:T(4,128)(2,1)S(1)} %collective-permute-done.6.refs_1_, bf16[2,16,4,256]{3,2,1,0:T(4,128)(2,1)S(1)} %collective-permute-done.7.refs_2_, ...), custom_call_target="tpu_custom_call" | custom-call | tf_op jit(solution)/shard_map/pallas_call | solution.py:153
  19.9 0.8 %collective-permute-done.5.refs_3_ = bf16[128,256]{1,0:T(8,128)(2,1)S(1)} collective-permute-done((bf16[128,256]{1,0:T(8,128)(2,1)S(1)}, bf16[128,256]{1,0:T(8,128)(2,1)S(1)}, u32[]{:S(2)}, u32[]{:S(2)}) %collective-permute-start.5) | collective-permute-done | bytes 65568 | tf_op jit(solution)/shard_map/ppermute | solution.py:28
  20.7 1.1 %shard_map.78 = (f32[2,64,256]{2,1,0:T(8,128)S(1)}, f32[128,256]{1,0:T(8,128)S(1)}, bf16[64,128]{1,0:T(8,128)(2,1)S(1)}, bf16[160,256]{1,0:T(8,128)(2,1)S(1)}, b...) custom-call(bf16[128,256]{1,0:T(8,128)(2,1)S(1)} %constant_dynamic-update-slice_fusion.refs_0_, ...), custom_call_target="tpu_custom_call" | custom-call | tf_op jit(solution)/shard_map/pallas_call | solution.py:153
  21.7 0.1 collective-permute-start.12
  21.8 3.6 %collective-permute-start.13 = (bf16[160,256]{1,0:T(8,128)(2,1)S(1)}, bf16[160,256]{1,0:T(8,128)(2,1)S(1)}, u32[]{:S(2)}, u32[]{:S(2)}) collective-permute-start(bf16[160,256]{1,0:T(8,128)(2,1)S(1)} %get-tuple-element.27), channel_id=1, source_target_pairs={{0,8},{4,12},{8,0},{12,4},{1,9},{5,13},{9,1},{13,5},{2,10},{6,14},... | collective-permute-start | bytes 245768 | tf_op jit(solution)/shard_map/ppermute | solution.py:28
  25.5 0.7 %collective-permute-start.14 = (bf16[160,256]{1,0:T(8,128)(2,1)S(1)}, bf16[160,256]{1,0:T(8,128)(2,1)S(1)}, u32[]{:S(2)}, u32[]{:S(2)}) collective-permute-start(bf16[160,256]{1,0:T(8,128)(2,1)S(1)} %get-tuple-element.28), channel_id=1, source_target_pairs={{0,12},{4,8},{8,4},{12,0},{1,13},{5,9},{9,5},{13,1},{2,14},{6,10},... | collective-permute-start | bytes 245768 | tf_op jit(solution)/shard_map/ppermute | solution.py:28
  26.2 0.9 %collective-permute-start.11 = (bf16[2,16,4,256]{3,2,1,0:T(4,128)(2,1)S(1)}, bf16[2,16,4,256]{3,2,1,0:T(4,128)(2,1)S(1)}, u32[]{:S(2)}, u32[]{:S(2)}) collective-permute-start(bf16[2,16,4,256]{3,2,1,0:T(4,128)(2,1)S(1)} %copy-done), channel_id=1, source_target_pairs={{0,3},{1,2},{2,1},{3,0},{4,7},{5,6},{6,5},{7,4},{8,11},{9,10},{10,... | collective-permute-start | bytes 196616 | tf_op jit(solution)/shard_map/ppermute | solution.py:28
  27.1 0.6 %collective-permute-start.9 = (bf16[2,16,4,256]{3,2,1,0:T(4,128)(2,1)S(1)}, bf16[2,16,4,256]{3,2,1,0:T(4,128)(2,1)S(1)}, u32[]{:S(2)}, u32[]{:S(2)}) collective-permute-start(bf16[2,16,4,256]{3,2,1,0:T(4,128)(2,1)S(1)} %copy-done), channel_id=1, source_target_pairs={{0,1},{1,0},{2,3},{3,2},{4,5},{5,4},{6,7},{7,6},{8,9},{9,8},{10,11... | collective-permute-start | bytes 196616 | tf_op jit(solution)/shard_map/ppermute | solution.py:28
  27.7 2.8 %collective-permute-done.11.refs_3_ = bf16[2,16,4,256]{3,2,1,0:T(4,128)(2,1)S(1)} collective-permute-done((bf16[2,16,4,256]{3,2,1,0:T(4,128)(2,1)S(1)}, bf16[2,16,4,256]{3,2,1,0:T(4,128)(2,1)S(1)}, u32[]{:S(2)}, u32[]{:S(2)}) %collective-permute-start.11) | collective-permute-done | bytes 65568 | tf_op jit(solution)/shard_map/ppermute | solution.py:28
  30.6 1.0 %shard_map.79.refs_2_ = bf16[4,4,32,512]{3,2,1,0:T(8,128)(2,1)S(1)} custom-call(s32[4]{0:T(128)} %bitcast.4, bf16[2,16,4,256]{3,2,1,0:T(4,128)(2,1)S(1)} %copy-done, bf16[2,16,4,256]{3,2,1,0:T(4,128)(2,1)S(1)} %collective-permute-done.9.refs_1_, bf16[2,16,4,256]{3,2,1,0:T(4,128)(2,1)S(1)} %collective-permute-done.10.refs_2_, ...), custom_call_target="tpu_custom_call" | custom-call | tf_op jit(solution)/shard_map/pallas_call | solution.py:153
  31.5 0.7 %copy.11 = f32[2,64,256]{2,1,0:T(8,128)} copy(f32[2,64,256]{2,1,0:T(8,128)S(1)} %get-tuple-element.31) | data formatting | bytes 262144
  32.2 0.1 collective-permute-done.13.refs_4_
  32.3 0.9 %shard_map.80 = (f32[2,64,256]{2,1,0:T(8,128)}, f32[2,64,256]{2,1,0:T(8,128)}) custom-call(f32[128,256]{1,0:T(8,128)S(1)} %get-tuple-element.24.refs_0_, bf16[64,128]{1,0:T(8,128)(2,1)S(1)} %get-tuple-element.25.refs_1_, bf16[4,4,32,512]{3,2,1,0:T(8,128)(2,1)S(1)} %shard_map.79.refs_2_, bf16[160,256]{1,0:T(8,128)(2,1)S(1)} %collective-permute-done.12.refs_3_, ...), custom_call_target="tpu_custom_call" | custom-call | tf_op jit(solution)/shard_map/pallas_call | solution.py:153
  (20 shorter events, 0.0 us)
Async XLA Ops:
  0.6 16.0 %collective-permute-start.6 = (bf16[2,16,4,256]{3,2,1,0:T(4,128)(2,1)}, bf16[2,16,4,256]{3,2,1,0:T(4,128)(2,1)S(1)}, u32[]{:S(2)}, u32[]{:S(2)}) collective-permute-start(bf16[2,16,4,256]{3,2,1,0:T(4,128)(2,1)} %refs_0_.2), channel_id=1, source_target_pairs={{0,1},{1,0},{2,3},{3,2},{4,5},{5,4},{6,7},{7,6},{8,9},{9,8},{10,11... | collective-permute-start | bytes 196616 | tf_op jit(solution)/shard_map/ppermute | solution.py:28
  1.2 15.8 %collective-permute-start.7 = (bf16[2,16,4,256]{3,2,1,0:T(4,128)(2,1)}, bf16[2,16,4,256]{3,2,1,0:T(4,128)(2,1)S(1)}, u32[]{:S(2)}, u32[]{:S(2)}) collective-permute-start(bf16[2,16,4,256]{3,2,1,0:T(4,128)(2,1)} %refs_0_.2), channel_id=1, source_target_pairs={{0,2},{1,3},{2,0},{3,1},{4,6},{5,7},{6,4},{7,5},{8,10},{9,11},{10,... | collective-permute-start | bytes 196616 | tf_op jit(solution)/shard_map/ppermute | solution.py:28
  3.7 15.4 %collective-permute-start.8 = (bf16[2,16,4,256]{3,2,1,0:T(4,128)(2,1)}, bf16[2,16,4,256]{3,2,1,0:T(4,128)(2,1)S(1)}, u32[]{:S(2)}, u32[]{:S(2)}) collective-permute-start(bf16[2,16,4,256]{3,2,1,0:T(4,128)(2,1)} %refs_0_.2), channel_id=1, source_target_pairs={{0,3},{1,2},{2,1},{3,0},{4,7},{5,6},{6,5},{7,4},{8,11},{9,10},{10,... | collective-permute-start | bytes 196616 | tf_op jit(solution)/shard_map/ppermute | solution.py:28
  5.1 4.5 %collective-permute-start = (bf16[32,256]{1,0:T(8,128)(2,1)S(1)}, bf16[32,256]{1,0:T(8,128)(2,1)S(1)}, u32[]{:S(2)}, u32[]{:S(2)}) collective-permute-start(bf16[32,256]{1,0:T(8,128)(2,1)S(1)} %get-tuple-element.18), channel_id=1, source_target_pairs={{0,4},{4,0},{8,12},{12,8},{1,5},{5,1},{9,13},{13,9},{2,6},{6,2},{1... | collective-permute-start | bytes 49160 | tf_op jit(solution)/shard_map/ppermute | solution.py:28
  6.9 5.8 %collective-permute-start.1 = (bf16[32,256]{1,0:T(8,128)(2,1)S(1)}, bf16[32,256]{1,0:T(8,128)(2,1)S(1)}, u32[]{:S(2)}, u32[]{:S(2)}) collective-permute-start(bf16[32,256]{1,0:T(8,128)(2,1)S(1)} %get-tuple-element.19), channel_id=1, source_target_pairs={{0,8},{4,12},{8,0},{12,4},{1,9},{5,13},{9,1},{13,5},{2,10},{6,14},... | collective-permute-start | bytes 49160 | tf_op jit(solution)/shard_map/ppermute | solution.py:28
  9.5 7.5 %copy-start = (bf16[2,16,4,256]{3,2,1,0:T(4,128)(2,1)S(1)}, bf16[2,16,4,256]{3,2,1,0:T(4,128)(2,1)}, u32[]{:S(2)}) copy-start(bf16[2,16,4,256]{3,2,1,0:T(4,128)(2,1)} %refs_0_.3) | copy-start | bytes 196612
  9.5 9.6 %copy-start.1 = (bf16[2,16,4,256]{3,2,1,0:T(4,128)(2,1)S(1)}, bf16[2,16,4,256]{3,2,1,0:T(4,128)(2,1)}, u32[]{:S(2)}) copy-start(bf16[2,16,4,256]{3,2,1,0:T(4,128)(2,1)} %refs_0_.2) | copy-start | bytes 196612
  9.5 5.6 %collective-permute-start.2 = (bf16[32,256]{1,0:T(8,128)(2,1)S(1)}, bf16[32,256]{1,0:T(8,128)(2,1)S(1)}, u32[]{:S(2)}, u32[]{:S(2)}) collective-permute-start(bf16[32,256]{1,0:T(8,128)(2,1)S(1)} %get-tuple-element.20), channel_id=1, source_target_pairs={{0,12},{4,8},{8,4},{12,0},{1,13},{5,9},{9,5},{13,1},{2,14},{6,10},... | collective-permute-start | bytes 49160 | tf_op jit(solution)/shard_map/ppermute | solution.py:28
  15.2 4.7 %collective-permute-start.3 = (bf16[128,256]{1,0:T(8,128)(2,1)S(1)}, bf16[128,256]{1,0:T(8,128)(2,1)S(1)}, u32[]{:S(2)}, u32[]{:S(2)}) collective-permute-start(bf16[128,256]{1,0:T(8,128)(2,1)S(1)} %constant_dynamic-update-slice_fusion.refs_0_), channel_id=1, source_target_pairs={{0,1},{1,0},{2,3},{3,2},{4,5},{5,4},{6,7},{7,6},{8,9},{9,8},{10,11... | collective-permute-start | bytes 196616 | tf_op jit(solution)/shard_map/ppermute | solution.py:28
  15.2 4.7 %collective-permute-start.4 = (bf16[128,256]{1,0:T(8,128)(2,1)S(1)}, bf16[128,256]{1,0:T(8,128)(2,1)S(1)}, u32[]{:S(2)}, u32[]{:S(2)}) collective-permute-start(bf16[128,256]{1,0:T(8,128)(2,1)S(1)} %constant_dynamic-update-slice_fusion.refs_0_), channel_id=1, source_target_pairs={{0,2},{1,3},{2,0},{3,1},{4,6},{5,7},{6,4},{7,5},{8,10},{9,11},{10,... | collective-permute-start | bytes 196616 | tf_op jit(solution)/shard_map/ppermute | solution.py:28
  16.7 4.0 %collective-permute-start.5 = (bf16[128,256]{1,0:T(8,128)(2,1)S(1)}, bf16[128,256]{1,0:T(8,128)(2,1)S(1)}, u32[]{:S(2)}, u32[]{:S(2)}) collective-permute-start(bf16[128,256]{1,0:T(8,128)(2,1)S(1)} %constant_dynamic-update-slice_fusion.refs_0_), channel_id=1, source_target_pairs={{0,3},{1,2},{2,1},{3,0},{4,7},{5,6},{6,5},{7,4},{8,11},{9,10},{10,... | collective-permute-start | bytes 196616 | tf_op jit(solution)/shard_map/ppermute | solution.py:28
  17.0 10.1 %collective-permute-start.10 = (bf16[2,16,4,256]{3,2,1,0:T(4,128)(2,1)S(1)}, bf16[2,16,4,256]{3,2,1,0:T(4,128)(2,1)S(1)}, u32[]{:S(2)}, u32[]{:S(2)}) collective-permute-start(bf16[2,16,4,256]{3,2,1,0:T(4,128)(2,1)S(1)} %copy-done), channel_id=1, source_target_pairs={{0,2},{1,3},{2,0},{3,1},{4,6},{5,7},{6,4},{7,5},{8,10},{9,11},{10,... | collective-permute-start | bytes 196616 | tf_op jit(solution)/shard_map/ppermute | solution.py:28
  21.7 10.4 %collective-permute-start.12 = (bf16[160,256]{1,0:T(8,128)(2,1)S(1)}, bf16[160,256]{1,0:T(8,128)(2,1)S(1)}, u32[]{:S(2)}, u32[]{:S(2)}) collective-permute-start(bf16[160,256]{1,0:T(8,128)(2,1)S(1)} %get-tuple-element.26), channel_id=1, source_target_pairs={{0,4},{4,0},{8,12},{12,8},{1,5},{5,1},{9,13},{13,9},{2,6},{6,2},{1... | collective-permute-start | bytes 245768 | tf_op jit(solution)/shard_map/ppermute | solution.py:28
  21.8 10.5 %collective-permute-start.13 = (bf16[160,256]{1,0:T(8,128)(2,1)S(1)}, bf16[160,256]{1,0:T(8,128)(2,1)S(1)}, u32[]{:S(2)}, u32[]{:S(2)}) collective-permute-start(bf16[160,256]{1,0:T(8,128)(2,1)S(1)} %get-tuple-element.27), channel_id=1, source_target_pairs={{0,8},{4,12},{8,0},{12,4},{1,9},{5,13},{9,1},{13,5},{2,10},{6,14},... | collective-permute-start | bytes 245768 | tf_op jit(solution)/shard_map/ppermute | solution.py:28
  25.5 6.9 %collective-permute-start.14 = (bf16[160,256]{1,0:T(8,128)(2,1)S(1)}, bf16[160,256]{1,0:T(8,128)(2,1)S(1)}, u32[]{:S(2)}, u32[]{:S(2)}) collective-permute-start(bf16[160,256]{1,0:T(8,128)(2,1)S(1)} %get-tuple-element.28), channel_id=1, source_target_pairs={{0,12},{4,8},{8,4},{12,0},{1,13},{5,9},{9,5},{13,1},{2,14},{6,10},... | collective-permute-start | bytes 245768 | tf_op jit(solution)/shard_map/ppermute | solution.py:28
  26.2 4.4 %collective-permute-start.11 = (bf16[2,16,4,256]{3,2,1,0:T(4,128)(2,1)S(1)}, bf16[2,16,4,256]{3,2,1,0:T(4,128)(2,1)S(1)}, u32[]{:S(2)}, u32[]{:S(2)}) collective-permute-start(bf16[2,16,4,256]{3,2,1,0:T(4,128)(2,1)S(1)} %copy-done), channel_id=1, source_target_pairs={{0,3},{1,2},{2,1},{3,0},{4,7},{5,6},{6,5},{7,4},{8,11},{9,10},{10,... | collective-permute-start | bytes 196616 | tf_op jit(solution)/shard_map/ppermute | solution.py:28
  27.1 3.4 %collective-permute-start.9 = (bf16[2,16,4,256]{3,2,1,0:T(4,128)(2,1)S(1)}, bf16[2,16,4,256]{3,2,1,0:T(4,128)(2,1)S(1)}, u32[]{:S(2)}, u32[]{:S(2)}) collective-permute-start(bf16[2,16,4,256]{3,2,1,0:T(4,128)(2,1)S(1)} %copy-done), channel_id=1, source_target_pairs={{0,1},{1,0},{2,3},{3,2},{4,5},{5,4},{6,7},{7,6},{8,9},{9,8},{10,11... | collective-permute-start | bytes 196616 | tf_op jit(solution)/shard_map/ppermute | solution.py:28

commit v3 on v2

--- a/solution.py
+++ b/solution.py
@@ -23,84 +23,143 @@
     return lax.dot_general(a, b, dims, preferred_element_type=F32)
 
 
-def swap(x, axis, step):
-    count = lax.axis_size(axis)
-    return lax.ppermute(x, axis, [(i, i ^ step) for i in range(count)])
+def swap(x, step):
+    count = lax.axis_size("rep")
+    return lax.ppermute(x, "rep", [(i, i ^ step) for i in range(count)])
+
+
+def cross(x, step, twist=0):
+    reps = lax.axis_size("rep")
+    count = lax.axis_size("tile") * reps
+    pairs = [(i, i ^ (step * reps) ^ (twist if i % 2 else 0)) for i in range(count)]
+    return lax.ppermute(x, ("tile", "rep"), pairs)
+
+
+LANES = 128
 
 
 def live_rows(ranks_ref, cell, shard, ranks):
     rows = lax.broadcasted_iota(jnp.int32, (ranks, 1), 0) + shard * ranks
-    return rows < ranks_ref[cell] * BUCKET
-
-
-def forward_kernel(ranks_ref, basis_ref, foc_ref, *refs):
-    ranks, tiles = basis_ref.shape[1], basis_ref.shape[2]
-    outs, blocks = refs[:tiles], refs[tiles]
+    return rows < ranks_ref[pl.ds(cell, 1), pl.ds(0, 1)] * BUCKET
+
+
+def fetch_kernel(ranks_in, keep_in, *refs):
+    count = (len(refs) - 4) // 2
+    arrays, live_out, outs = refs[:count], refs[count], refs[count + 1 : 2 * count + 1]
+    ranks_ref, keep_ref, sems = refs[2 * count + 1 :]
+    scalars = [
+        pltpu.make_async_copy(ranks_in, ranks_ref, sems.at[count]),
+        pltpu.make_async_copy(keep_in, keep_ref, sems.at[count + 1]),
+    ]
+    copies = [pltpu.make_async_copy(ref, out, sems.at[i]) for i, (ref, out) in enumerate(zip(arrays, outs))]
+    for copy in scalars + copies:
+        copy.start()
+    for copy in scalars:
+        copy.wait()
+    tiles = ranks_in.shape[0]
+    for cell in range(tiles):
+        live_out[pl.ds(cell, 1), :] = jnp.full((1, LANES), ranks_ref[cell], jnp.int32)
+    live_out[pl.ds(tiles, 1), :] = jnp.full((1, LANES), keep_ref[0], jnp.int32)
+    for copy in copies:
+        copy.wait()
+
+
+def forward_kernel(ranks_ref, own_ref, pair_ref, lift_ref, foc_ref, *refs):
+    ranks, tiles = own_ref.shape[1], own_ref.shape[2]
+    outs, bundle, blocks = refs[:tiles], refs[tiles], refs[tiles + 1]
     here = lax.axis_index("tile")
-    shard = lax.axis_index("rep")
+    me = lax.axis_index("rep")
+    core = lax.rem(me, 2)
     points = foc_ref.shape[0] // 2
-    rows = [basis_ref[part, :, cell, :] for cell in range(tiles) for part in range(2)]
+    pieces = (own_ref, pair_ref)
+    rows = [ref[part, :, cell, :] for cell in range(tiles) for ref in pieces for part in range(2)]
     prod = dot(jnp.concatenate(rows, axis=0), foc_ref[...], NT)
     for cell in range(tiles):
-        mask = live_rows(ranks_ref, cell, shard, ranks)
-        real = prod[2 * cell * ranks : (2 * cell + 1) * ranks]
-        imag = prod[(2 * cell + 1) * ranks : (2 * cell + 2) * ranks]
-        coef = [real[:, :points] - imag[:, points:], real[:, points:] + imag[:, :points]]
-        for part in range(2):
-            blocks[cell, pl.ds(part * ranks, ranks), :] = jnp.where(mask, coef[part], 0.0).astype(BF16)
+        for shard in range(2):
+            mask = live_rows(ranks_ref, cell, me ^ shard, ranks)
+            first = (cell * 2 + shard) * 2 * ranks
+            real = prod[first : first + ranks]
+            imag = prod[first + ranks : first + 2 * ranks]
+            coef = [real[:, :points] - imag[:, points:], real[:, points:] + imag[:, :points]]
+            for part in range(2):
+                spot = pl.multiple_of(((core ^ shard) * 2 + part) * ranks, ranks)
+                blocks[cell, pl.ds(spot, ranks), :] = jnp.where(mask, coef[part], 0.0).astype(BF16)
     for step in range(tiles):
         outs[step][...] = blocks[here ^ step]
-
-
-def lift_kernel(keep_ref, *refs, reps):
-    pieces, out, weight = refs[:reps], refs[reps], refs[reps + 1]
-    ranks, tiles, width = pieces[0].shape[1:]
+    size = 2 * ranks
+    bundle[pl.ds(0, size)] = lift_ref[...].reshape(size, tiles, points)
+    bundle[pl.ds(size, size)] = own_ref[...].reshape(size, tiles, points)
+    own = blocks[here, pl.ds(pl.multiple_of(core * size, size), size), :]
+    bundle[pl.ds(2 * size, size // tiles)] = own.reshape(size // tiles, tiles, points)
+
+
+def put_lift(out, spot, slot, real, imag):
+    ranks, width = real.shape
+    out[spot, slot, pl.ds(0, ranks), pl.ds(0, width)] = real
+    out[spot, slot, pl.ds(0, ranks), pl.ds(width, width)] = imag
+    out[spot, slot, pl.ds(ranks, ranks), pl.ds(0, width)] = -imag
+    out[spot, slot, pl.ds(ranks, ranks), pl.ds(width, width)] = real
+
+
+def lift_kernel(live_ref, own_ref, pair_ref, far_ref, out, weight):
+    ranks, tiles, width = own_ref.shape[1:]
     here = lax.axis_index("tile")
+    core = lax.rem(lax.axis_index("rep"), 2)
     columns = lax.broadcasted_iota(jnp.int32, weight.shape, 1)
     columns = jnp.where(columns >= width, columns - width, columns)
-    weight[...] = (columns < keep_ref[0]).astype(F32)
-    for shard in range(reps):
-        for cell in range(tiles):
-            real = pieces[shard][0, :, cell, :]
-            imag = pieces[shard][1, :, cell, :]
-            spot = here ^ cell
-            out[spot, shard, pl.ds(0, ranks), pl.ds(0, width)] = real
-            out[spot, shard, pl.ds(0, ranks), pl.ds(width, width)] = imag
-            out[spot, shard, pl.ds(ranks, ranks), pl.ds(0, width)] = -imag
-            out[spot, shard, pl.ds(ranks, ranks), pl.ds(width, width)] = real
-
-
-def image_basis_kernel(ranks_ref, *refs, reps):
-    pieces, out = refs[:reps], refs[reps]
-    ranks, tiles, width = pieces[0].shape[1:]
+    weight[...] = (columns < live_ref[pl.ds(tiles, 1), pl.ds(0, 1)]).astype(F32)
+    for cell in range(tiles):
+        spot = here ^ cell
+        put_lift(out, spot, core, own_ref[0, :, cell, :], own_ref[1, :, cell, :])
+        put_lift(out, spot, 1 - core, pair_ref[0, :, cell, :], pair_ref[1, :, cell, :])
+        put_lift(out, spot, 2 + core, far_ref[pl.ds(0, ranks), cell, :], far_ref[pl.ds(ranks, ranks), cell, :])
+
+
+def image_basis_kernel(ranks_ref, own_ref, pair_ref, far_ref, last_ref, out):
+    ranks, tiles, width = own_ref.shape[1:]
+    size = 2 * ranks
     here = lax.axis_index("tile")
     me = lax.axis_index("rep")
-    for shard in range(reps):
-        for cell in range(tiles):
-            mask = live_rows(ranks_ref, cell, me ^ shard, ranks)
-            real = jnp.where(mask, pieces[shard][0, :, cell, :].astype(F32), 0.0)
-            imag = jnp.where(mask, pieces[shard][1, :, cell, :].astype(F32), 0.0)
-            spot = here ^ cell
-            out[spot, shard, pl.ds(0, ranks), pl.ds(0, width)] = real.astype(BF16)
-            out[spot, shard, pl.ds(0, ranks), pl.ds(width, width)] = (-imag).astype(BF16)
-            out[spot, shard, pl.ds(ranks, ranks), pl.ds(0, width)] = imag.astype(BF16)
-            out[spot, shard, pl.ds(ranks, ranks), pl.ds(width, width)] = real.astype(BF16)
-
-
-def middle_kernel(*refs, tiles, reps, factor):
-    pieces, lift_ref, weight_ref = refs[:reps], refs[reps], refs[reps + 1]
-    fwd_out, own_corr, own_back = refs[reps + 2], refs[reps + 3], refs[reps + 4]
-    sends, whole = refs[reps + 5 : reps + 4 + tiles], refs[reps + 4 + tiles]
+    core = lax.rem(me, 2)
+    for cell in range(tiles):
+        pieces = [(core, me, own_ref[0, :, cell, :], own_ref[1, :, cell, :])]
+        pieces.append((1 - core, me ^ 1, pair_ref[0, :, cell, :], pair_ref[1, :, cell, :]))
+        for slot, shard, ref in ((2 + core, me ^ 2, far_ref), (3 - core, me ^ 3, last_ref)):
+            parts = [ref[pl.ds(size + part * ranks, ranks), cell, :] for part in range(2)]
+            pieces.append((slot, shard, *parts))
+        spot = here ^ cell
+        for slot, shard, real, imag in pieces:
+            mask = live_rows(ranks_ref, cell, shard, ranks)
+            real = jnp.where(mask, real.astype(F32), 0.0)
+            imag = jnp.where(mask, imag.astype(F32), 0.0)
+            out[spot, slot, pl.ds(0, ranks), pl.ds(0, width)] = real.astype(BF16)
+            out[spot, slot, pl.ds(0, ranks), pl.ds(width, width)] = (-imag).astype(BF16)
+            out[spot, slot, pl.ds(ranks, ranks), pl.ds(0, width)] = imag.astype(BF16)
+            out[spot, slot, pl.ds(ranks, ranks), pl.ds(width, width)] = real.astype(BF16)
+
+
+def middle_kernel(near_ref, far_ref, last_ref, mine_ref, pair_ref, lift_in, weight_ref, *refs, factor):
+    lift_ref, fwd_out, own_corr, own_back = refs[:4]
+    tiles, reps, block, width2 = lift_ref.shape
+    sends, whole, coef = refs[4 : 3 + tiles], refs[3 + tiles], refs[4 + tiles]
     me = lax.axis_index("rep")
-    points, width2 = whole.shape
+    core = lax.rem(me, 2)
+    here = lax.axis_index("tile")
+    points = whole.shape[0]
     width = width2 // 2
     share = points // reps
-    block = lift_ref.shape[2]
-    total = None
-    for shard in range(reps):
-        lift = lift_ref[:, shard].reshape(tiles * block, width2)
-        part = dot(pieces[shard][...], lift, TN)
-        total = part if total is None else total + part
+    ranks = block // 2
+    for cell in range(tiles):
+        put_lift(
+            lift_ref, here ^ cell, 3 - core, last_ref[pl.ds(0, ranks), cell, :], last_ref[pl.ds(ranks, ranks), cell, :]
+        )
+    coef[0, pl.ds(0, 2)] = near_ref[...].reshape(2, block, points)
+    coef[0, 2 + core] = far_ref[pl.ds(2 * block, block // tiles)].reshape(block, points)
+    coef[0, 3 - core] = last_ref[pl.ds(2 * block, block // tiles)].reshape(block, points)
+    coef[pl.ds(1, tiles - 1), pl.ds(2 * core, 2)] = mine_ref[...].reshape(tiles - 1, 2, block, points)
+    coef[pl.ds(1, tiles - 1), pl.ds(2 - 2 * core, 2)] = pair_ref[...].reshape(tiles - 1, 2, block, points)
+    rows = tiles * reps * block
+    total = dot(coef[...].reshape(rows, points), lift_ref[...].reshape(rows, width2), TN)
     whole[...] = total
     mine = whole[pl.ds(pl.multiple_of(me * share, share), share), :]
     fwd_out[0] = mine[:, :width]
@@ -147,15 +206,17 @@
     corr_out[1] = corr[share:]
 
 
-def call(kernel, ins, outs, scratch, args):
+def call(kernel, ins, outs, scratch, args, aliases={}):
     vmem, smem = pl.BlockSpec(memory_space=pltpu.VMEM), pl.BlockSpec(memory_space=pltpu.SMEM)
+    kinds = {"s": smem, "h": pl.BlockSpec(memory_space=pl.ANY), "p": vmem}
     args = [pltpu.with_memory_space_constraint(a, pltpu.VMEM) if k == "p" else a for k, a in zip(ins, args)]
     return pl.pallas_call(
         kernel,
-        in_specs=[smem if kind == "s" else vmem for kind in ins],
+        in_specs=[kinds[kind] for kind in ins],
         out_specs=[vmem] * len(outs),
         out_shape=outs,
         scratch_shapes=scratch,
+        input_output_aliases=aliases,
     )(*args)
 
 
@@ -168,44 +229,57 @@
     factor = 1.0 / math.sqrt(SPAN * width * tiles)
     shaped, placed = jax.ShapeDtypeStruct, pltpu.VMEM
     order = sorted(range(1, tiles), reverse=True)
-    rep_order = sorted(range(1, reps), key=lambda s: (s == 1, s))
-    live = tile_ranks.reshape(tiles)
-
+
+    source_pair = swap(source, 1)
+    live, source, receiver, foc = call(
+        fetch_kernel,
+        "hhhhh",
+        [
+            placed((8, LANES), jnp.int32),
+            placed(source.shape, BF16),
+            placed(receiver.shape, BF16),
+            placed((2 * points, width), BF16),
+        ],
+        [pltpu.SMEM((tiles,), jnp.int32), pltpu.SMEM((1,), jnp.int32), pltpu.SemaphoreType.DMA((5,))],
+        (tile_ranks.reshape(tiles), keep_counts, source, receiver, focusing.reshape(2 * points, width)),
+    )
     made = call(
         forward_kernel,
-        "svv",
-        [placed((block, points), BF16)] * tiles,
-        [pltpu.VMEM((tiles, block, points), BF16)],
-        (live, source, focusing.reshape(2 * points, width)),
-    )
-    got = {step: swap(made[step], "tile", step) for step in order}
-    lifts = {step: swap(receiver, "rep", step) for step in rep_order}
-    gathered = jnp.concatenate([made[0]] + [got[step] for step in range(1, tiles)], axis=0)
-    spread = {step: swap(gathered, "rep", step) for step in rep_order}
-    bases = {step: swap(source, "rep", step) for step in rep_order}
+        "ppppp",
+        [placed((2 * block, points), BF16)] * tiles + [placed((2 * block + block // tiles, tiles, points), BF16)],
+        [pltpu.VMEM((tiles, 2 * block, points), BF16)],
+        (live, source, source_pair, receiver, foc),
+    )
+    far = swap(made[tiles], 2)
+    got = {step: cross(made[step], step, 2) for step in order}
+    receiver_pair = swap(receiver, 1)
+    last = swap(far, 1)
+    gathered = jnp.concatenate([got[step] for step in range(1, tiles)], axis=0)
+    spread = swap(gathered, 1)
     lift, weight = call(
-        functools.partial(lift_kernel, reps=reps),
-        "s" + "p" * reps,
+        lift_kernel,
+        "pppp",
         [placed((tiles, reps, block, 2 * width), BF16), placed((8, 2 * width), F32)],
         [],
-        (keep_counts, receiver, *[lifts[step] for step in range(1, reps)]),
+        (live, receiver, receiver_pair, far),
     )
     middle = call(
-        functools.partial(middle_kernel, tiles=tiles, reps=reps, factor=factor),
-        "p" * (reps + 2),
-        [placed((2, share, width), F32), placed((2 * share, points), F32), placed((share, reps * block), BF16)]
+        functools.partial(middle_kernel, factor=factor),
+        "ppppppp",
+        [placed(lift.shape, BF16), placed((2, share, width), F32), placed((2 * share, points), F32), placed((share, reps * block), BF16)]
         + [placed((2 * share + share // 2, points), BF16)] * (tiles - 1),
-        [pltpu.VMEM((points, 2 * width), F32)],
-        (gathered, *[spread[step] for step in range(1, reps)], lift, weight),
-    )
-    forward_data, own_corr, own_back = middle[:3]
-    sent = {step: swap(middle[2 + step], "tile", step) for step in order}
+        [pltpu.VMEM((points, 2 * width), F32), pltpu.VMEM((tiles, reps, block, points), BF16)],
+        (made[0], far, last, gathered, spread, lift, weight),
+        {5: 0},
+    )
+    forward_data, own_corr, own_back = middle[1:4]
+    sent = {step: cross(middle[3 + step], step) for step in order}
     (basis,) = call(
-        functools.partial(image_basis_kernel, reps=reps),
-        "s" + "p" * reps,
+        image_basis_kernel,
+        "ppppp",
         [placed((tiles, reps, block, 2 * width), BF16)],
         [],
-        (live, source, *[bases[step] for step in range(1, reps)]),
+        (live, source, source_pair, far, last),
     )
     adjoint, corr = call(
         functools.partial(final_kernel, tiles=tiles, reps=reps),
@@ -258,13 +332,9 @@
     return forward_data, adjoint, lax.psum(corr, "tile")
 
 
-def power_of_two(n):
-    return n & (n - 1) == 0
-
-
 def solution(mesh):
     tiles, reps = mesh.shape["tile"], mesh.shape["rep"]
-    short = tiles <= 4 and power_of_two(tiles) and power_of_two(reps)
+    short = tiles == 4 and reps == 4
 
     def per_device(*args):
         return (short_path if short else long_path)(*args)

time: 33.4 us -> 29.9 us (0.90)
  starting transfers between devices: 20.1 us -> 12.5 us
  waiting for transfers between devices: 6.21 us -> 11 us
  Pallas kernels: 4.81 us -> 4.25 us
    ppermute x15 -> x11, starting transfers between devices: 20.1 us -> 12.5 us  [the longest x6 9.89 us: cross(): return lax.ppermute(x, ('tile', 'rep'), pairs)]
    ppermute x15 -> x11, waiting for transfers between devices: 6.21 us -> 11 us  [the longest x6 9.93 us: cross(): return lax.ppermute(x, ('tile', 'rep'), pairs)]
    pallas_call x5 -> x6, Pallas kernels: 4.81 us -> 4.25 us  [call(): pl.pallas_call(kernel, in_specs=[kinds[kind] for kind in ins], out_specs=...]
    unnamed x8 -> x3, local copies, waits for them, and re-layouts: 0.67 us -> 0.66 us
  transfers between devices with their start and end apart: 15 -> 11, of which waited for: 4 -> 5; matrix products, arithmetic and copies ran while one was open for 2% -> 2% of each run, Pallas kernels for 12% -> 6%
where the time goes in v3:
time: 29.9 us; the launch traced here: 29.8 us
  starting transfers between devices  12.5 us (42%)
  waiting for transfers between devices  11 us (37%)
  Pallas kernels  4.25 us (14%)
  between operations  1.36 us (5%)
  local copies, waits for them, and re-layouts  0.66 us (2%)
    ppermute x6, waiting for transfers between devices, cross(): return lax.ppermute(x, ('tile', 'rep'), pairs)  9.93 us
    ppermute x6, starting transfers between devices, cross(): return lax.ppermute(x, ('tile', 'rep'), pairs)  9.89 us
    pallas_call x6, Pallas kernels, call(): pl.pallas_call(kernel, in_specs=[kinds[kind] for kind in ins], out_specs=...  4.25 us
    ppermute x5, starting transfers between devices, swap(): return lax.ppermute(x, 'rep', [(i, i ^ step) for i in range(count)])  2.62 us
    ppermute x5, waiting for transfers between devices, swap(): return lax.ppermute(x, 'rep', [(i, i ^ step) for i in range(count)])  1.07 us
    unnamed x3, local copies, waits for them, and re-layouts  0.66 us
  transfers between devices with their start and end apart: 11, of which 5 were waited for; matrix products, arithmetic and copies ran while one was open for 2% of the time, Pallas kernels for 6%

profile of v3, /device:TPU:0, one launch (start us, length us, event | category | flops | bytes accessed | tf_op | source)
XLA Modules:
  0.0 29.8 jit_solution(13909455686159627314)
XLA Ops:
  0.6 0.6 %collective-permute-start = (bf16[2,16,4,256]{3,2,1,0:T(4,128)(2,1)}, bf16[2,16,4,256]{3,2,1,0:T(4,128)(2,1)S(1)}, u32[]{:S(2)}, u32[]{:S(2)}) collective-permute-start(bf16[2,16,4,256]{3,2,1,0:T(4,128)(2,1)} %refs_0_.1), channel_id=1, source_target_pairs={{0,1},{1,0},{2,3},{3,2},{4,5},{5,4},{6,7},{7,6},{8,9},{9,8},{10,11... | collective-permute-start | bytes 196616 | tf_op jit(solution)/shard_map/ppermute | solution.py:28
  1.8 1.1 %shard_map.76 = (s32[8,128]{1,0:T(8,128)S(1)}, bf16[2,16,4,256]{3,2,1,0:T(4,128)(2,1)S(1)}, bf16[2,16,4,256]{3,2,1,0:T(4,128)(2,1)S(1)}, bf16[512,256]{1,0:T(8,128)(2,1)S(1)}) custom-call(s32[4]{0:T(128)} %bitcast.3, s32[1]{0:T(128)S(6)} %copy.13.keep_in, bf16[2,16,4,256]{3,2,1,0:T(4,128)(2,1)} %refs_0_.1, bf16[2,16,4,256]{3,2,1,0:T(4,128)(2,1)} %refs_1_.1, ...), custom_call_target="tpu_custom_call" | custom-call | tf_op jit(solution)/shard_map/pallas_call | solution.py:213
  2.9 0.0 collective-permute-done.pair_ref
  2.9 0.4 %shard_map.77 = (bf16[64,256]{1,0:T(8,128)(2,1)S(1)}, bf16[64,256]{1,0:T(8,128)(2,1)S(1)}, bf16[64,256]{1,0:T(8,128)(2,1)S(1)}, bf16[64,256]{1,0:T(8,128)(2,1)S(1)}, bf16[72,4,256]{2,1,0:T(4,128)(2,1)S(1)}) custom-call(s32[8,128]{1,0:T(8,128)S(1)} %get-tuple-element.22.ranks_ref.live_ref, bf16[2,16,4,256]{3,2,1,0:T(4,128)(2,1)S(1)} %get-tuple-element.23.own_ref, ...), custom_call_target="tpu_custom_call" | custom-call | tf_op jit(solution)/shard_map/pallas_call | solution.py:213
  3.3 2.6 %collective-permute-start.3 = (bf16[64,256]{1,0:T(8,128)(2,1)S(1)}, bf16[64,256]{1,0:T(8,128)(2,1)S(1)}, u32[]{:S(2)}, u32[]{:S(2)}) collective-permute-start(bf16[64,256]{1,0:T(8,128)(2,1)S(1)} %get-tuple-element.28), channel_id=1, source_target_pairs={{0,4},{1,7},{2,6},{3,5},{4,0},{5,3},{6,2},{7,1},{8,12},{9,15},{10,... | collective-permute-start | bytes 98312 | tf_op jit(solution)/shard_map/ppermute | solution.py:35
  6.0 1.5 %collective-permute-start.1 = (bf16[72,4,256]{2,1,0:T(4,128)(2,1)S(1)}, bf16[72,4,256]{2,1,0:T(4,128)(2,1)S(1)}, u32[]{:S(2)}, u32[]{:S(2)}) collective-permute-start(bf16[72,4,256]{2,1,0:T(4,128)(2,1)S(1)} %get-tuple-element.27), channel_id=1, source_target_pairs={{0,2},{1,3},{2,0},{3,1},{4,6},{5,7},{6,4},{7,5},{8,10},{9,11},{10,... | collective-permute-start | bytes 442376 | tf_op jit(solution)/shard_map/ppermute | solution.py:28
  7.5 2.6 %collective-permute-start.4 = (bf16[64,256]{1,0:T(8,128)(2,1)S(1)}, bf16[64,256]{1,0:T(8,128)(2,1)S(1)}, u32[]{:S(2)}, u32[]{:S(2)}) collective-permute-start(bf16[64,256]{1,0:T(8,128)(2,1)S(1)} %get-tuple-element.29), channel_id=1, source_target_pairs={{0,8},{1,11},{2,10},{3,9},{4,12},{5,15},{6,14},{7,13},{8,0},{9,3},... | collective-permute-start | bytes 98312 | tf_op jit(solution)/shard_map/ppermute | solution.py:35
  10.1 0.2 collective-permute-start.5
  10.3 2.8 %collective-permute-done.4 = bf16[64,256]{1,0:T(8,128)(2,1)S(1)} collective-permute-done((bf16[64,256]{1,0:T(8,128)(2,1)S(1)}, bf16[64,256]{1,0:T(8,128)(2,1)S(1)}, u32[]{:S(2)}, u32[]{:S(2)}) %collective-permute-start.4) | collective-permute-done | bytes 32800 | tf_op jit(solution)/shard_map/ppermute | solution.py:35
  13.1 0.1 collective-permute-start.2
  13.2 2.6 %collective-permute-done.5 = bf16[64,256]{1,0:T(8,128)(2,1)S(1)} collective-permute-done((bf16[64,256]{1,0:T(8,128)(2,1)S(1)}, bf16[64,256]{1,0:T(8,128)(2,1)S(1)}, u32[]{:S(2)}, u32[]{:S(2)}) %collective-permute-start.5) | collective-permute-done | bytes 32800 | tf_op jit(solution)/shard_map/ppermute | solution.py:35
  15.8 0.3 %collective-permute-start.6 = (bf16[192,256]{1,0:T(8,128)(2,1)S(1)}, bf16[192,256]{1,0:T(8,128)(2,1)S(1)}, u32[]{:S(2)}, u32[]{:S(2)}) collective-permute-start(bf16[192,256]{1,0:T(8,128)(2,1)S(1)} %constant_dynamic-update-slice_fusion.mine_ref), channel_id=1, source_target_pairs={{0,1},{1,0},{2,3},{3,2},{4,5},{5,4},{6,7},{7,6},{8,9},{9,8},{10,11... | collective-permute-start | bytes 294920 | tf_op jit(solution)/shard_map/ppermute | solution.py:28
  16.1 0.2 collective-permute-start.7
  16.3 1.1 %collective-permute-done.7.pair_ref = bf16[2,16,4,256]{3,2,1,0:T(4,128)(2,1)S(1)} collective-permute-done((bf16[2,16,4,256]{3,2,1,0:T(4,128)(2,1)S(1)}, bf16[2,16,4,256]{3,2,1,0:T(4,128)(2,1)S(1)}, u32[]{:S(2)}, u32[]{:S(2)}) %collective-permute-start.7) | collective-permute-done | bytes 65568 | tf_op jit(solution)/shard_map/ppermute | solution.py:28
  17.3 0.6 %shard_map.78 = (bf16[4,4,32,512]{3,2,1,0:T(8,128)(2,1)S(1)}, f32[8,512]{1,0:T(8,128)S(1)}) custom-call(s32[8,128]{1,0:T(8,128)S(1)} %get-tuple-element.22.ranks_ref.live_ref, bf16[2,16,4,256]{3,2,1,0:T(4,128)(2,1)S(1)} %get-tuple-element.24.lift_ref.own_ref, bf16[2,16,4,256]{3,2,1,0:T(4,128)(2,1)S(1)} %collective-permute-done.7.pair_ref, ...), custom_call_target="tpu_custom_call" | custom-call | tf_op jit(solution)/shard_map/pallas_call | solution.py:213
  17.9 1.1 %shard_map.79 = (bf16[4,4,32,512]{3,2,1,0:T(8,128)(2,1)S(1)}, f32[2,64,256]{2,1,0:T(8,128)S(1)}, f32[128,256]{1,0:T(8,128)S(1)}, bf16[64,128]{1,0:T(8,128)(2,1)S...) custom-call(bf16[64,256]{1,0:T(8,128)(2,1)S(1)} %get-tuple-element.2, ...), custom_call_target="tpu_custom_call", output_to_operand_aliasing={{0}: (5, {})} | custom-call | tf_op jit(solution)/shard_map/pallas_call | solution.py:213
  19.0 0.1 collective-permute-start.8
  19.1 1.4 %collective-permute-start.9 = (bf16[160,256]{1,0:T(8,128)(2,1)S(1)}, bf16[160,256]{1,0:T(8,128)(2,1)S(1)}, u32[]{:S(2)}, u32[]{:S(2)}) collective-permute-start(bf16[160,256]{1,0:T(8,128)(2,1)S(1)} %get-tuple-element.37), channel_id=1, source_target_pairs={{0,8},{1,9},{2,10},{3,11},{4,12},{5,13},{6,14},{7,15},{8,0},{9,1},... | collective-permute-start | bytes 245768 | tf_op jit(solution)/shard_map/ppermute | solution.py:35
  20.5 3.0 %collective-permute-start.10 = (bf16[160,256]{1,0:T(8,128)(2,1)S(1)}, bf16[160,256]{1,0:T(8,128)(2,1)S(1)}, u32[]{:S(2)}, u32[]{:S(2)}) collective-permute-start(bf16[160,256]{1,0:T(8,128)(2,1)S(1)} %get-tuple-element.38), channel_id=1, source_target_pairs={{0,12},{1,13},{2,14},{3,15},{4,8},{5,9},{6,10},{7,11},{8,4},{9,5},... | collective-permute-start | bytes 245768 | tf_op jit(solution)/shard_map/ppermute | solution.py:35
  23.4 0.7 %copy.12 = f32[2,64,256]{2,1,0:T(8,128)} copy(f32[2,64,256]{2,1,0:T(8,128)S(1)} %get-tuple-element.41) | data formatting | bytes 262144
  24.1 0.3 %shard_map.80.refs_2_ = bf16[4,4,32,512]{3,2,1,0:T(8,128)(2,1)S(1)} custom-call(s32[8,128]{1,0:T(8,128)S(1)} %get-tuple-element.22.ranks_ref.live_ref, bf16[2,16,4,256]{3,2,1,0:T(4,128)(2,1)S(1)} %get-tuple-element.23.own_ref, bf16[2,16,4,256]{3,2,1,0:T(4,128)(2,1)S(1)} %collective-permute-done.pair_ref, ...), custom_call_target="tpu_custom_call" | custom-call | tf_op jit(solution)/shard_map/pallas_call | solution.py:213
  24.4 0.3 collective-permute-done.8.refs_3_
  24.7 4.2 %collective-permute-done.9.refs_4_ = bf16[160,256]{1,0:T(8,128)(2,1)S(1)} collective-permute-done((bf16[160,256]{1,0:T(8,128)(2,1)S(1)}, bf16[160,256]{1,0:T(8,128)(2,1)S(1)}, u32[]{:S(2)}, u32[]{:S(2)}) %collective-permute-start.9) | collective-permute-done | bytes 81952 | tf_op jit(solution)/shard_map/ppermute | solution.py:35
  28.9 0.9 %shard_map.81 = (f32[2,64,256]{2,1,0:T(8,128)}, f32[2,64,256]{2,1,0:T(8,128)}) custom-call(f32[128,256]{1,0:T(8,128)S(1)} %get-tuple-element.34.refs_0_, bf16[64,128]{1,0:T(8,128)(2,1)S(1)} %get-tuple-element.35.refs_1_, bf16[4,4,32,512]{3,2,1,0:T(8,128)(2,1)S(1)} %shard_map.80.refs_2_, bf16[160,256]{1,0:T(8,128)(2,1)S(1)} %collective-permute-done.8.refs_3_, ...), custom_call_target="tpu_custom_call" | custom-call | tf_op jit(solution)/shard_map/pallas_call | solution.py:213
  (8 shorter events, 0.0 us)
Async XLA Ops:
  0.6 2.3 %collective-permute-start = (bf16[2,16,4,256]{3,2,1,0:T(4,128)(2,1)}, bf16[2,16,4,256]{3,2,1,0:T(4,128)(2,1)S(1)}, u32[]{:S(2)}, u32[]{:S(2)}) collective-permute-start(bf16[2,16,4,256]{3,2,1,0:T(4,128)(2,1)} %refs_0_.1), channel_id=1, source_target_pairs={{0,1},{1,0},{2,3},{3,2},{4,5},{5,4},{6,7},{7,6},{8,9},{9,8},{10,11... | collective-permute-start | bytes 196616 | tf_op jit(solution)/shard_map/ppermute | solution.py:28
  3.3 6.9 %collective-permute-start.3 = (bf16[64,256]{1,0:T(8,128)(2,1)S(1)}, bf16[64,256]{1,0:T(8,128)(2,1)S(1)}, u32[]{:S(2)}, u32[]{:S(2)}) collective-permute-start(bf16[64,256]{1,0:T(8,128)(2,1)S(1)} %get-tuple-element.28), channel_id=1, source_target_pairs={{0,4},{1,7},{2,6},{3,5},{4,0},{5,3},{6,2},{7,1},{8,12},{9,15},{10,... | collective-permute-start | bytes 98312 | tf_op jit(solution)/shard_map/ppermute | solution.py:35
  6.0 7.1 %collective-permute-start.1 = (bf16[72,4,256]{2,1,0:T(4,128)(2,1)S(1)}, bf16[72,4,256]{2,1,0:T(4,128)(2,1)S(1)}, u32[]{:S(2)}, u32[]{:S(2)}) collective-permute-start(bf16[72,4,256]{2,1,0:T(4,128)(2,1)S(1)} %get-tuple-element.27), channel_id=1, source_target_pairs={{0,2},{1,3},{2,0},{3,1},{4,6},{5,7},{6,4},{7,5},{8,10},{9,11},{10,... | collective-permute-start | bytes 442376 | tf_op jit(solution)/shard_map/ppermute | solution.py:28
  7.5 5.6 %collective-permute-start.4 = (bf16[64,256]{1,0:T(8,128)(2,1)S(1)}, bf16[64,256]{1,0:T(8,128)(2,1)S(1)}, u32[]{:S(2)}, u32[]{:S(2)}) collective-permute-start(bf16[64,256]{1,0:T(8,128)(2,1)S(1)} %get-tuple-element.29), channel_id=1, source_target_pairs={{0,8},{1,11},{2,10},{3,9},{4,12},{5,15},{6,14},{7,13},{8,0},{9,3},... | collective-permute-start | bytes 98312 | tf_op jit(solution)/shard_map/ppermute | solution.py:35
  10.1 5.7 %collective-permute-start.5 = (bf16[64,256]{1,0:T(8,128)(2,1)S(1)}, bf16[64,256]{1,0:T(8,128)(2,1)S(1)}, u32[]{:S(2)}, u32[]{:S(2)}) collective-permute-start(bf16[64,256]{1,0:T(8,128)(2,1)S(1)} %get-tuple-element.30), channel_id=1, source_target_pairs={{0,12},{1,15},{2,14},{3,13},{4,8},{5,11},{6,10},{7,9},{8,4},{9,7},... | collective-permute-start | bytes 98312 | tf_op jit(solution)/shard_map/ppermute | solution.py:35
  13.1 4.8 %collective-permute-start.2 = (bf16[72,4,256]{2,1,0:T(4,128)(2,1)S(1)}, bf16[72,4,256]{2,1,0:T(4,128)(2,1)S(1)}, u32[]{:S(2)}, u32[]{:S(2)}) collective-permute-start(bf16[72,4,256]{2,1,0:T(4,128)(2,1)S(1)} %collective-permute-done.1.far_ref), channel_id=1, source_target_pairs={{0,1},{1,0},{2,3},{3,2},{4,5},{5,4},{6,7},{7,6},{8,9},{9,8},{10,11... | collective-permute-start | bytes 442376 | tf_op jit(solution)/shard_map/ppermute | solution.py:28
  15.8 2.1 %collective-permute-start.6 = (bf16[192,256]{1,0:T(8,128)(2,1)S(1)}, bf16[192,256]{1,0:T(8,128)(2,1)S(1)}, u32[]{:S(2)}, u32[]{:S(2)}) collective-permute-start(bf16[192,256]{1,0:T(8,128)(2,1)S(1)} %constant_dynamic-update-slice_fusion.mine_ref), channel_id=1, source_target_pairs={{0,1},{1,0},{2,3},{3,2},{4,5},{5,4},{6,7},{7,6},{8,9},{9,8},{10,11... | collective-permute-start | bytes 294920 | tf_op jit(solution)/shard_map/ppermute | solution.py:28
  16.1 1.3 %collective-permute-start.7 = (bf16[2,16,4,256]{3,2,1,0:T(4,128)(2,1)S(1)}, bf16[2,16,4,256]{3,2,1,0:T(4,128)(2,1)S(1)}, u32[]{:S(2)}, u32[]{:S(2)}) collective-permute-start(bf16[2,16,4,256]{3,2,1,0:T(4,128)(2,1)S(1)} %get-tuple-element.24.lift_ref.own_ref), channel_id=1, source_target_pairs={{0,1},{1,0},{2,3},{3,2},{4,5},{5,4},{6,7},{7,6},{8,9},{9,8},{10,11... | collective-permute-start | bytes 196616 | tf_op jit(solution)/shard_map/ppermute | solution.py:28
  19.0 5.7 %collective-permute-start.8 = (bf16[160,256]{1,0:T(8,128)(2,1)S(1)}, bf16[160,256]{1,0:T(8,128)(2,1)S(1)}, u32[]{:S(2)}, u32[]{:S(2)}) collective-permute-start(bf16[160,256]{1,0:T(8,128)(2,1)S(1)} %get-tuple-element.36), channel_id=1, source_target_pairs={{0,4},{1,5},{2,6},{3,7},{4,0},{5,1},{6,2},{7,3},{8,12},{9,13},{10,... | collective-permute-start | bytes 245768 | tf_op jit(solution)/shard_map/ppermute | solution.py:35
  19.1 9.8 %collective-permute-start.9 = (bf16[160,256]{1,0:T(8,128)(2,1)S(1)}, bf16[160,256]{1,0:T(8,128)(2,1)S(1)}, u32[]{:S(2)}, u32[]{:S(2)}) collective-permute-start(bf16[160,256]{1,0:T(8,128)(2,1)S(1)} %get-tuple-element.37), channel_id=1, source_target_pairs={{0,8},{1,9},{2,10},{3,11},{4,12},{5,13},{6,14},{7,15},{8,0},{9,1},... | collective-permute-start | bytes 245768 | tf_op jit(solution)/shard_map/ppermute | solution.py:35
  20.5 8.4 %collective-permute-start.10 = (bf16[160,256]{1,0:T(8,128)(2,1)S(1)}, bf16[160,256]{1,0:T(8,128)(2,1)S(1)}, u32[]{:S(2)}, u32[]{:S(2)}) collective-permute-start(bf16[160,256]{1,0:T(8,128)(2,1)S(1)} %get-tuple-element.38), channel_id=1, source_target_pairs={{0,12},{1,13},{2,14},{3,15},{4,8},{5,9},{6,10},{7,11},{8,4},{9,5},... | collective-permute-start | bytes 245768 | tf_op jit(solution)/shard_map/ppermute | solution.py:35
